TPU v7x, 32 devices: a whole 2x2x4 slice. The times are simulated.
32 devices in a mesh: leaf: 8 (over z, y), sub: 4 (over x, core).
Axes of the slice: x: 2, y: 2, z: 4, core: 2. Of those that a mesh axis runs over, the one named last changes fastest.
Arguments:
- sources: bfloat16 [65536, 64], P(('leaf', 'sub')), may hold values from -6 to 6
- leaf_basis: bfloat16 [256, 256, 64], P(('leaf', 'sub')), may hold values from -0.375 to 0.375
- transfer: float32 [2, 64, 64], replicated, may hold values from -0.625 to 0.625
- coupling: float32 [3, 64, 64], replicated, may hold values from -0.5 to 0.5
- near_blocks: bfloat16 [256, 4, 256, 256], P(('leaf', 'sub')), may hold values from -0.1875 to 0.1875
- near_pattern: int32 [256, 4], P(('leaf', 'sub')), may hold values from 0 to 255, as said below
- far_pattern: int32 [508, 3], replicated, may hold values 0 or 1
Outputs:
- product: bfloat16 [65536, 64], P(('leaf', 'sub'))
Inputs may be any that keep to these rules, and one draw needn't show every extreme that they name: near_pattern[i, 0] = i; every entry j has j // 8 - i // 8 equal to 0, 1, -1, 4 or -4.
All inputs are finite; a program needn't handle non-finite values.
Results may differ from a plain program's by a relative error of at most 0.001.
Values may be sent and summed in bfloat16 or wider, within the bound.
A program may use at most 64 MiB of HBM per device.

v0:
```python
import functools

import jax
import jax.numpy as jnp
from jax import lax
from jax.experimental import pallas as pl
from jax.experimental.pallas import tpu as pltpu
from jax.sharding import PartitionSpec as P

BF = jnp.bfloat16
F32 = jnp.float32
MESH = pl.DeviceIdType.MESH


def halves(x):
    hi = x.astype(BF)
    return hi, (x - hi.astype(F32)).astype(BF)


def split(x):
    return jnp.concatenate(halves(x), axis=1)


def nt(a, b):
    return lax.dot_general(a, b, (((1,), (1,)), ((), ())), preferred_element_type=F32)


def nn(a, b):
    return jnp.dot(a, b, preferred_element_type=F32)


def fold(y, width):
    return y[:, :width] + y[:, width:]


def kernel(
    cfg, src, basis, transfer, coupling, blocks, near_pat, far_pat, out,
    buf, bas, nb, buf_a, pair2, buf4, buf5, buf6, wdown, wpath,
    load_sem, nb_sem, halo_send, near_recv, y_recv, z_recv, a_send, a_recv, p_send, p_recv,
    b_send, b_recv, q_send, q_recv, known,
):
    sub, devices, leaf_dev, near = cfg
    rank = basis.shape[1]
    rhs = src.shape[0]
    points = basis.shape[2]
    block = 2 * sub
    block_count = devices // block
    me = lax.axis_index("leaf") * sub + lax.axis_index("sub")
    mine = lax.rem(me, block)
    own_block = me // block
    place_sub = lax.rem(me, sub)
    upper = mine // sub

    def target(dev):
        return (dev // sub, lax.rem(dev, sub))

    def remote(source, dest, send, recv, dev):
        return pltpu.make_async_remote_copy(
            src_ref=source, dst_ref=dest, send_sem=send, recv_sem=recv,
            device_id=target(dev), device_id_type=MESH,
        )

    barrier = pltpu.get_barrier_semaphore()
    peers = []
    for k in range(1, block):
        peers.append(own_block * block + lax.rem(mine + k, block))

    def greet(semaphore, condition, peer):
        @pl.when(condition)
        def _():
            pl.semaphore_signal(semaphore, inc=1, device_id=target(peer), device_id_type=MESH)

    greet(barrier, own_block > 0, me - block)
    greet(barrier, own_block < block_count - 1, me + block)
    for peer in peers:
        pl.semaphore_signal(barrier, inc=1, device_id=target(peer), device_id_type=MESH)

    rounds = block_count - 2

    def make_known(r):
        greet(known.at[r - 1, 0], (own_block > 0) & (own_block + r < block_count), me - block)
        greet(known.at[r - 1, 1], (own_block < block_count - 1) & (own_block >= r), me + block)

    def get_known(r):
        @pl.when(own_block + r + 1 < block_count)
        def _():
            pl.semaphore_wait(known.at[r - 1, 0], 1)

        @pl.when(own_block >= r + 1)
        def _():
            pl.semaphore_wait(known.at[r - 1, 1], 1)

    loads = [
        pltpu.make_async_copy(
            src.at[:, pl.ds(points * leaf, points)], buf.at[2, leaf], load_sem.at[leaf]
        )
        for leaf in range(leaf_dev)
    ]
    base_load = pltpu.make_async_copy(basis, bas, load_sem.at[leaf_dev])
    base_load.start()
    for copy in loads:
        copy.start()
    near_loads = [
        pltpu.make_async_copy(blocks.at[leaf], nb.at[leaf], nb_sem.at[leaf])
        for leaf in range(leaf_dev)
    ]
    for copy in near_loads:
        copy.start()

    def doubled(parts):
        rows = []
        for part in parts:
            row = split(part)
            rows += [row, row]
        return jnp.concatenate(rows, axis=0)

    sides = [transfer[side] for side in range(2)]
    step_weight = jnp.concatenate([doubled([side]) for side in sides], axis=1)
    w_up = {2: doubled(sides)}
    paths = sides
    while len(paths) < max(leaf_dev, block):
        wide = nn(split(jnp.concatenate(paths, axis=0)), step_weight)
        longer = jnp.concatenate(
            [fold(wide[:, : 2 * rank], rank), fold(wide[:, 2 * rank :], rank)], axis=0
        )
        paths = [longer[p * rank : (p + 1) * rank] for p in range(2 * len(paths))]
        w_up[len(paths)] = doubled(paths)

    def lift(parts, span):
        rows = [
            jnp.concatenate(parts[p * span : (p + 1) * span], axis=1)
            for p in range(len(parts) // span)
        ]
        rows = rows[0] if len(rows) == 1 else jnp.concatenate(rows, axis=0)
        lifted = split(fold(nn(rows, w_up[span]), rank))
        return [lifted[p * rhs : (p + 1) * rhs] for p in range(len(parts) // span)]

    base_load.wait()
    for copy in loads:
        copy.wait()
    moment0 = [split(nt(buf[2, leaf], bas[leaf])) for leaf in range(leaf_dev)]
    buf_a[mine] = lift(moment0, leaf_dev)[0]
    two = lift(moment0, leaf_dev // 2)
    pair2[0, 0] = two[0]
    pair2[0, 1] = two[1]

    ends = jnp.where(own_block > 0, 1, 0) + jnp.where(own_block < block_count - 1, 1, 0)
    pl.semaphore_wait(barrier, len(peers) + ends)
    a_copies = []
    for k in range(block - 1, 0, -1):
        a_copies.append(
            remote(
                buf_a.at[mine], buf_a.at[mine], a_send.at[k], a_recv.at[k],
                own_block * block + lax.rem(mine + k, block),
            )
        )
    for copy in a_copies:
        copy.start()
    pair_copy = remote(
        pair2.at[0], pair2.at[1], p_send.at[0], p_recv.at[0], me + 1 - 2 * lax.rem(me, 2)
    )
    pair_copy.start()

    if rounds > 0:
        make_known(1)

    y_slot = 4 - 4 * upper
    z_slot = 4 * upper
    across = me + sub - 2 * sub * upper

    def send_across():
        for leaf in range(leaf_dev):
            remote(
                src.at[:, pl.ds(points * leaf, points)], buf.at[z_slot, leaf],
                halo_send.at[0], y_recv.at[leaf], across,
            ).start()

    outer = (place_sub == 0) | (place_sub == sub - 1)
    pl.when(outer)(send_across)
    for number, step in enumerate((1, -1)):
        @pl.when(place_sub < sub - 1 if step > 0 else place_sub > 0)
        def _(number=number, step=step):
            for leaf in range(leaf_dev):
                remote(
                    src.at[:, pl.ds(points * leaf, points)], buf.at[2 - step, leaf],
                    halo_send.at[1 + number], near_recv.at[number], me + step,
                ).start()

    z_step = block - 2 * block * upper
    z_target = me + z_step
    z_send = (z_target >= 0) & (z_target < devices)
    z_have = (me - z_step >= 0) & (me - z_step < devices)
    first_turn = ((upper == 0) & (place_sub == 0)) | ((upper == 1) & (place_sub == sub - 1))
    second_turn = z_have & (
        ((upper == 0) & (place_sub == sub - 1)) | ((upper == 1) & (place_sub == 0))
    )

    def turn(slot, leaf):
        @pl.when(place_sub == 0)
        def _():
            remote(
                buf.at[slot, leaf], buf.at[3, leaf],
                halo_send.at[4], near_recv.at[1], me + sub - 1,
            ).start()

        @pl.when(place_sub == sub - 1)
        def _():
            remote(
                buf.at[slot, leaf], buf.at[1, leaf],
                halo_send.at[4], near_recv.at[0], me - sub + 1,
            ).start()

    def relay_first(leaf):
        remote(
            buf.at[y_slot, leaf], buf.at[y_slot, leaf], halo_send.at[0], y_recv.at[leaf], across
        ).wait_recv()

        @pl.when(z_send)
        def _():
            remote(
                buf.at[y_slot, leaf], buf.at[z_slot, leaf],
                halo_send.at[3], z_recv.at[leaf], z_target,
            ).start()

        @pl.when(first_turn)
        def _():
            turn(y_slot, leaf)

    def z_wait(leaf):
        remote(
            buf.at[z_slot, leaf], buf.at[z_slot, leaf], halo_send.at[3], z_recv.at[leaf], across
        ).wait_recv()

    def relay_second(leaf):
        @pl.when(second_turn)
        def _():
            z_wait(leaf)
            turn(z_slot, leaf)

    row_starts = [0]
    size = leaf_dev * devices
    while size > 4:
        row_starts.append(row_starts[-1] + size)
        size //= 2

    def weight(offset, row):
        return jnp.full((rhs, 2 * rank), far_pat[offset, row].astype(F32), F32).astype(BF)

    c_hi, c_lo = [], []
    for offset in range(3):
        hi, lo = halves(coupling[offset])
        c_hi += [hi, hi]
        c_lo += [lo, lo]
    w_couple = jnp.concatenate(
        [jnp.concatenate(c_hi, axis=1), jnp.concatenate(c_lo, axis=1)], axis=0
    )

    def couple(groups, rows):
        stacked = [
            jnp.concatenate(
                [weight(offset, row) * members[offset] for offset in range(3)], axis=1
            )
            for members, row in zip(groups, rows)
        ]
        stacked = stacked[0] if len(stacked) == 1 else jnp.concatenate(stacked, axis=0)
        return fold(nt(stacked, w_couple), rank)

    for side in range(2):
        hi, lo = halves(sides[side])
        wdown[side] = jnp.concatenate(
            [jnp.concatenate([hi, hi], axis=1), jnp.concatenate([lo, lo], axis=1)], axis=0
        )
    w_down = jnp.concatenate([wdown[0], wdown[1]], axis=0)

    def descend(field, step):
        return fold(nt(split(field), wdown[lax.rem(me >> step, 2)]), rank)

    def fan_out(field, rows):
        both = nt(split(field), w_down)
        children = []
        for p in range(field.shape[0] // rows):
            row = both[p * rows : (p + 1) * rows]
            children.append(fold(row[:, : 2 * rank], rank))
            children.append(fold(row[:, 2 * rank :], rank))
        return jnp.concatenate(children, axis=0)

    low_levels = leaf_dev.bit_length() - 1
    top_count = len(row_starts) - low_levels - 2
    eye = (
        lax.broadcasted_iota(jnp.int32, (rank, rank), 0)
        == lax.broadcasted_iota(jnp.int32, (rank, rank), 1)
    ).astype(F32)
    chain = eye
    for step in range(top_count, -1, -1):
        if step <= 1:
            chain = descend(chain, step)
        elif step < top_count + 1:
            chain = jnp.concatenate([descend(chain, step), eye], axis=0)
    for _ in range(low_levels):
        chain = fan_out(chain, top_count * rank)
    for leaf in range(leaf_dev):
        for number in range(top_count):
            begin = (leaf * top_count + number) * rank
            piece = split(chain[begin : begin + rank])
            for half in range(2):
                wpath[
                    (2 * number + half) * rank : (2 * number + half + 1) * rank,
                    2 * rank * leaf : 2 * rank * (leaf + 1),
                ] = piece

    def relays(early, late):
        @pl.when(outer)
        def _():
            for step, leaf in early:
                step(leaf)

        if late:
            @pl.when(jnp.logical_not(outer))
            def _():
                for leaf in late:
                    relay_first(leaf)

    queue = [(relay_first, leaf) for leaf in range(leaf_dev)]
    queue += [(relay_second, leaf) for leaf in range(leaf_dev)]
    half = leaf_dev // 2
    relays(queue[:half], [])

    locals_low = []
    level_vals, level_id = moment0, 0
    while (leaf_dev >> level_id) >= 4:
        if level_id:
            level_vals = lift(level_vals, 2)
        count = leaf_dev >> level_id
        locals_low.append(
            couple(
                [
                    [level_vals[c // 4 * 4 + (c + offset) % 4] for offset in range(1, 4)]
                    for c in range(count)
                ],
                [row_starts[level_id] + me * count + c for c in range(count)],
            )
        )
        level_id += 1

    for r in range(1, rounds + 1):
        get_known(r)
        if r < rounds:
            make_known(r + 1)

    for k in range(block - 1, 0, -1):
        source = lax.rem(mine - k + block, block)
        remote(
            buf_a.at[source], buf_a.at[source], a_send.at[k], a_recv.at[k], me ^ 1
        ).wait_recv()
    eight = [buf_a[p] for p in range(block)]
    buf6[own_block] = lift(eight, block)[0]
    b_copies = []
    for k in range(block_count - 1, 0, -1):
        b_copies.append(
            remote(
                buf6.at[own_block], buf6.at[own_block], b_send.at[k], b_recv.at[k],
                lax.rem(own_block + k, block_count) * block + mine,
            )
        )
    for copy in b_copies:
        copy.start()
    five = lift(eight, block // 2)
    for p in range(2):
        buf5[p] = five[p]
    q_copy = remote(
        buf5.at[pl.ds(0, 2)], buf5.at[pl.ds(2, 2)], q_send.at[0], q_recv.at[0],
        (own_block + 1 - 2 * lax.rem(own_block, 2)) * block + mine,
    )
    q_copy.start()
    pl.when(jnp.logical_not(outer))(send_across)
    relays(queue[half:leaf_dev], [])
    for p, part in enumerate(lift(eight, 2)):
        buf4[p] = part

    pair_copy.wait()
    members2 = two + [pair2[1, 0], pair2[1, 1]]
    groups = [[members2[(c + offset) % 4] for offset in range(1, 4)] for c in range(2)]
    rows = [row_starts[level_id] + me * 2 + c for c in range(2)]
    level_id += 1
    groups.append(
        [buf_a[upper * sub + lax.rem(place_sub + offset, 4)] for offset in range(1, 4)]
    )
    rows.append(row_starts[level_id] + me)
    groups.append([buf4[lax.rem(mine // 2 + offset, 4)] for offset in range(1, 4)])
    rows.append(row_starts[level_id + 1] + me // 2)
    relays(queue[leaf_dev : leaf_dev + 2], range(0, 2))
    middle = couple(groups, rows)
    locals_low.append(middle[: 2 * rhs])
    field = middle[2 * rhs : 3 * rhs] + descend(middle[3 * rhs :], 0)
    for step in range(len(locals_low) - 1, -1, -1):
        field = locals_low[step] + fan_out(field, rhs)
    relays(queue[leaf_dev + 2 : leaf_dev + half], range(2, half))

    for copy in near_loads:
        copy.wait()
    first = [nt(buf[2, leaf], nb[leaf, 0]) for leaf in range(leaf_dev)]
    relays(queue[leaf_dev + half :], range(half, leaf_dev))

    for k in range(block_count - 1, 0, -1):
        source = lax.rem(own_block - k + block_count, block_count)
        remote(
            buf6.at[source], buf6.at[source], b_send.at[k], b_recv.at[k], me ^ 1
        ).wait_recv()
    q_copy.wait()
    groups = [[buf5[lax.rem(upper + offset, 4)] for offset in range(1, 4)]]
    rows = [row_starts[level_id + 2] + me // sub]
    first_six = level_id + 3
    start, span, level = 0, block_count, first_six
    while True:
        own = own_block >> (level - first_six)
        groups.append(
            [
                buf6[start + own // 4 * 4 + lax.rem(lax.rem(own, 4) + offset, 4)]
                for offset in range(1, 4)
            ]
        )
        rows.append(row_starts[level] + own)
        if span <= 4:
            break
        for p, part in enumerate(lift([buf6[start + p] for p in range(span)], 2)):
            buf6[start + span + p] = part
        start, span, level = start + span, span // 2, level + 1
    groups, rows = groups[::-1], rows[::-1]
    top = split(couple(groups, rows))
    top = jnp.concatenate([top[p * rhs : (p + 1) * rhs] for p in range(top_count)], axis=1)
    spread = nn(top, wpath[...])
    partial = []
    for leaf in range(leaf_dev):
        whole = split(
            field[leaf * rhs : (leaf + 1) * rhs]
            + fold(spread[:, 2 * rank * leaf : 2 * rank * (leaf + 1)], rank)
        )
        twice = jnp.concatenate([bas[leaf], bas[leaf]], axis=0)
        partial.append(first[leaf] + nn(whole, twice))

    @pl.when(z_have & jnp.logical_not(second_turn))
    def _():
        for leaf in range(leaf_dev):
            z_wait(leaf)

    for number, step in enumerate((-1, 1)):
        @pl.when(me > 0 if step < 0 else me < devices - 1)
        def _(number=number, step=step):
            pltpu.make_async_copy(buf.at[2 + step], buf.at[2 + step], near_recv.at[number]).wait()
    for leaf in range(leaf_dev):
        acc = partial[leaf]
        for s in range(1, near):
            index = near_pat[s, leaf]
            gap = index // leaf_dev - me
            place = jnp.where(
                gap == -sub, 0, jnp.where(gap == -1, 1, jnp.where(gap == 0, 2, jnp.where(gap == 1, 3, 4)))
            )
            acc = acc + nt(buf[place, lax.rem(index, leaf_dev)], nb[leaf, s])
        out[:, points * leaf : points * (leaf + 1)] = acc.astype(out.dtype)

    sent = (
        me >= 0, place_sub < sub - 1, place_sub > 0, z_send, first_turn | second_turn,
    )
    for number, condition in enumerate(sent):
        @pl.when(condition)
        def _(number=number):
            pltpu.make_async_copy(buf.at[2], buf.at[2], halo_send.at[number]).wait()
    for copy in a_copies + b_copies:
        copy.wait_send()


def shards(sizes, sources, leaf_basis, transfer, coupling, near_blocks, near_pattern, far_pattern):
    sub, devices = sizes
    leaf_dev, points, rank = leaf_basis.shape
    rhs = sources.shape[1]
    near = near_blocks.shape[1]
    block = 2 * sub
    block_count = devices // block
    top_count = block_count.bit_length() - 1
    vmem = pl.BlockSpec(memory_space=pltpu.VMEM)
    smem = pl.BlockSpec(memory_space=pltpu.SMEM)
    hbm = pl.BlockSpec(memory_space=pl.ANY)
    dma = pltpu.SemaphoreType.DMA
    result = pl.pallas_call(
        functools.partial(kernel, (sub, devices, leaf_dev, near)),
        out_shape=pltpu.VMEM((rhs, leaf_dev * points), BF),
        in_specs=[hbm, hbm, vmem, vmem, hbm, smem, smem],
        out_specs=vmem,
        scratch_shapes=[
            pltpu.VMEM((5, leaf_dev, rhs, points), BF),
            pltpu.VMEM((leaf_dev, rank, points), BF),
            pltpu.VMEM((leaf_dev, near, points, points), BF),
            pltpu.VMEM((block, rhs, 2 * rank), BF),
            pltpu.VMEM((2, 2, rhs, 2 * rank), BF),
            pltpu.VMEM((4, rhs, 2 * rank), BF),
            pltpu.VMEM((4, rhs, 2 * rank), BF),
            pltpu.VMEM((2 * block_count, rhs, 2 * rank), BF),
            pltpu.VMEM((2, 2 * rank, 2 * rank), BF),
            pltpu.VMEM((2 * top_count * rank, 2 * rank * leaf_dev), BF),
            dma((leaf_dev + 1,)),
            dma((leaf_dev,)),
            dma((5,)),
            dma((2,)),
            dma((leaf_dev,)),
            dma((leaf_dev,)),
            dma((block,)),
            dma((block,)),
            dma((1,)),
            dma((1,)),
            dma((block_count,)),
            dma((block_count,)),
            dma((1,)),
            dma((1,)),
            pltpu.SemaphoreType.REGULAR((max(block_count - 2, 1), 2)),
        ],
        compiler_params=pltpu.CompilerParams(collective_id=0, has_side_effects=True),
    )(
        sources.T,
        leaf_basis.transpose(0, 2, 1),
        transfer,
        coupling,
        near_blocks,
        near_pattern.T,
        far_pattern.T,
    )
    return result.T


def solution(mesh):
    placed = (
        P(("leaf", "sub"), None),
        P(("leaf", "sub"), None, None),
        P(),
        P(),
        P(("leaf", "sub"), None, None, None),
        P(("leaf", "sub"), None),
        P(),
    )
    sizes = (mesh.shape["sub"], mesh.shape["leaf"] * mesh.shape["sub"])
    return jax.shard_map(
        functools.partial(shards, sizes),
        mesh=mesh, in_specs=placed, out_specs=P(("leaf", "sub"), None), check_vma=False,
    )
```

profile of v0, /device:TPU:23, one launch (start us, length us, event | category | flops | bytes accessed | tf_op | source)
XLA Modules:
  0.0 22.1 jit_solution(5065929700500254295)
XLA Ops:
  0.0 21.3 %shard_map.73 = bf16[64,2048]{1,0:T(8,128)(2,1)S(1)} custom-call(bf16[64,2048]{1,0:T(8,128)(2,1)} %bitcast.6, bf16[8,64,256]{2,1,0:T(8,128)(2,1)} %bitcast.7, f32[2,64,64]{2,1,0:T(8,128)} %transfer.1, f32[3,64,64]{2,1,0:T(8,128)} %coupling.1, bf16[8,4,256,256]{3,2,1,0:T(8,128)(2,1)} %blocks.1, s32[4,8]{1,0:T(4,128)} %bitcast.9, s32[3,508]{1,0:T(4,128)} %bitcast.8), custom_call_target="tpu_custom_call" | custom-call | tf_op jit(solution)/shard_map/pallas_call | solution.py:484
  21.3 0.7 %copy.9 = bf16[2048,64]{0,1:T(8,128)(2,1)} copy(bf16[2048,64]{0,1:T(8,128)(2,1)S(1)} %bitcast.5) | data formatting | bytes 524288
where the time goes:
time: 22.3 us; the launch traced here: 22.1 us
  Pallas kernels  21.3 us (96%)
  local copies, waits for them, and re-layouts  0.71 us (3%)
    pallas_call x1, Pallas kernels, shards(): pl.pallas_call(functools.partial(kernel, (sub, devices, leaf_dev, near)),...  21.3 us
    unnamed x1, local copies, waits for them, and re-layouts  0.71 us

commit v1 on v0

--- a/solution.py
+++ b/solution.py
@@ -1,4 +1,5 @@
 import functools
+from contextlib import nullcontext
 
 import jax
 import jax.numpy as jnp
@@ -12,6 +13,10 @@
 MESH = pl.DeviceIdType.MESH
 
 
+def mark(name):
+    return nullcontext()
+
+
 def halves(x):
     hi = x.astype(BF)
     return hi, (x - hi.astype(F32)).astype(BF)
@@ -34,10 +39,10 @@
 
 
 def kernel(
-    cfg, src, basis, transfer, coupling, blocks, near_pat, far_pat, out,
-    buf, bas, nb, buf_a, pair2, buf4, buf5, buf6, wdown, wpath,
-    load_sem, nb_sem, halo_send, near_recv, y_recv, z_recv, a_send, a_recv, p_send, p_recv,
-    b_send, b_recv, q_send, q_recv, known,
+    cfg, src, basis, transfer_hbm, coupling_hbm, blocks, near_hbm, far_hbm, out,
+    buf, bas, nb, buf_a, pair2, buf4, buf5, buf6, wdown, wpath, transfer, coupling,
+    near_pat, far_pat, load_sem, halo_send, near_recv, y_recv, z_recv, a_sem, p_sem,
+    b_sem, q_sem, known,
 ):
     sub, devices, leaf_dev, near = cfg
     rank = basis.shape[1]
@@ -50,6 +55,29 @@
     own_block = me // block
     place_sub = lax.rem(me, sub)
     upper = mine // sub
+    has_prev = own_block > 0
+    has_next = own_block < block_count - 1
+    first_sub, last_sub = place_sub == 0, place_sub == sub - 1
+    outer = first_sub | last_sub
+    lower = upper == 0
+    relayed = leaf_dev // 2
+    turned = leaf_dev // 2
+    head = leaf_dev // 4
+
+    y_slot = 4 - 4 * upper
+    z_slot = 4 * upper
+    across = me + sub - 2 * sub * upper
+    z_step = block - 2 * block * upper
+    z_target = me + z_step
+    z_send = (lower & has_next) | (jnp.logical_not(lower) & has_prev)
+    z_have = (lower & has_prev) | (jnp.logical_not(lower) & has_next)
+    beyond = me - sub + 2 * sub * upper
+    first_turn = (lower & first_sub) | (jnp.logical_not(lower) & last_sub)
+    other_turn = (lower & last_sub) | (jnp.logical_not(lower) & first_sub)
+    second_turn = z_have & other_turn
+    skip_turn = z_send & other_turn
+    skip_target = z_target + (sub - 1) * (2 * upper - 1)
+    skip_source = me - (z_step + (sub - 1) * (2 * upper - 1))
 
     def target(dev):
         return (dev // sub, lax.rem(dev, sub))
@@ -70,10 +98,33 @@
         def _():
             pl.semaphore_signal(semaphore, inc=1, device_id=target(peer), device_id_type=MESH)
 
-    greet(barrier, own_block > 0, me - block)
-    greet(barrier, own_block < block_count - 1, me + block)
+    expected = len(peers) + sum(
+        jnp.where(condition, 1, 0) for condition in (has_prev, has_next, z_have, skip_turn)
+    )
     for peer in peers:
         pl.semaphore_signal(barrier, inc=1, device_id=target(peer), device_id_type=MESH)
+    greet(barrier, has_prev, me - block)
+    greet(barrier, has_next, me + block)
+    greet(barrier, z_have, beyond)
+    greet(barrier, z_have & first_turn, skip_source)
+
+    small_loads = [
+        pltpu.make_async_copy(source, dest, load_sem.at[number])
+        for number, (source, dest) in enumerate(
+            (
+                (transfer_hbm, transfer), (coupling_hbm, coupling),
+                (near_hbm, near_pat), (far_hbm, far_pat), (basis, bas),
+            )
+        )
+    ]
+    for copy in small_loads[:1] + small_loads[4:]:
+        copy.start()
+    for leaf in range(leaf_dev):
+        pltpu.make_async_copy(
+            src.at[:, pl.ds(points * leaf, points)], buf.at[2, leaf], load_sem.at[5]
+        ).start()
+    for copy in small_loads[1:4]:
+        copy.start()
 
     rounds = block_count - 2
 
@@ -89,23 +140,6 @@
         @pl.when(own_block >= r + 1)
         def _():
             pl.semaphore_wait(known.at[r - 1, 1], 1)
-
-    loads = [
-        pltpu.make_async_copy(
-            src.at[:, pl.ds(points * leaf, points)], buf.at[2, leaf], load_sem.at[leaf]
-        )
-        for leaf in range(leaf_dev)
-    ]
-    base_load = pltpu.make_async_copy(basis, bas, load_sem.at[leaf_dev])
-    base_load.start()
-    for copy in loads:
-        copy.start()
-    near_loads = [
-        pltpu.make_async_copy(blocks.at[leaf], nb.at[leaf], nb_sem.at[leaf])
-        for leaf in range(leaf_dev)
-    ]
-    for copy in near_loads:
-        copy.start()
 
     def doubled(parts):
         rows = []
@@ -114,6 +148,8 @@
             rows += [row, row]
         return jnp.concatenate(rows, axis=0)
 
+    with mark("00tc"):
+        small_loads[0].wait()
     sides = [transfer[side] for side in range(2)]
     step_weight = jnp.concatenate([doubled([side]) for side in sides], axis=1)
     w_up = {2: doubled(sides)}
@@ -135,48 +171,45 @@
         lifted = split(fold(nn(rows, w_up[span]), rank))
         return [lifted[p * rhs : (p + 1) * rhs] for p in range(len(parts) // span)]
 
-    base_load.wait()
-    for copy in loads:
-        copy.wait()
-    moment0 = [split(nt(buf[2, leaf], bas[leaf])) for leaf in range(leaf_dev)]
-    buf_a[mine] = lift(moment0, leaf_dev)[0]
-    two = lift(moment0, leaf_dev // 2)
-    pair2[0, 0] = two[0]
-    pair2[0, 1] = two[1]
-
-    ends = jnp.where(own_block > 0, 1, 0) + jnp.where(own_block < block_count - 1, 1, 0)
-    pl.semaphore_wait(barrier, len(peers) + ends)
-    a_copies = []
-    for k in range(block - 1, 0, -1):
-        a_copies.append(
-            remote(
-                buf_a.at[mine], buf_a.at[mine], a_send.at[k], a_recv.at[k],
-                own_block * block + lax.rem(mine + k, block),
-            )
-        )
-    for copy in a_copies:
-        copy.start()
-    pair_copy = remote(
-        pair2.at[0], pair2.at[1], p_send.at[0], p_recv.at[0], me + 1 - 2 * lax.rem(me, 2)
-    )
-    pair_copy.start()
-
-    if rounds > 0:
-        make_known(1)
-
-    y_slot = 4 - 4 * upper
-    z_slot = 4 * upper
-    across = me + sub - 2 * sub * upper
-
-    def send_across():
-        for leaf in range(leaf_dev):
+    def send_across(leaves):
+        for leaf in leaves:
             remote(
                 src.at[:, pl.ds(points * leaf, points)], buf.at[z_slot, leaf],
                 halo_send.at[0], y_recv.at[leaf], across,
             ).start()
 
-    outer = (place_sub == 0) | (place_sub == sub - 1)
-    pl.when(outer)(send_across)
+    def send_inner():
+        send_across(range(relayed))
+        for leaf in range(relayed, leaf_dev):
+            @pl.when(z_have)
+            def _(leaf=leaf):
+                remote(
+                    src.at[:, pl.ds(points * leaf, points)], buf.at[y_slot, leaf],
+                    halo_send.at[5], z_recv.at[leaf], beyond,
+                ).start()
+
+            send_across([leaf])
+
+    with mark("03barrier"):
+        pl.semaphore_wait(barrier, expected)
+    pl.when(outer)(functools.partial(send_across, range(head)))
+    with mark("01load"):
+        small_loads[4].wait()
+        pltpu.make_async_copy(buf.at[2], buf.at[2], load_sem.at[5]).wait()
+    with mark("02mom"):
+        moment0 = [split(nt(buf[2, leaf], bas[leaf])) for leaf in range(leaf_dev)]
+        buf_a[mine] = lift(moment0, leaf_dev)[0]
+    with mark("04asend"):
+        for k in range(block - 1, 0, -1):
+            remote(
+                buf_a.at[mine], buf_a.at[mine], a_sem.at[0], a_sem.at[1],
+                own_block * block + lax.rem(mine + k, block),
+            ).start()
+
+    if rounds > 0:
+        make_known(1)
+
+    pl.when(outer)(functools.partial(send_across, range(head, leaf_dev)))
     for number, step in enumerate((1, -1)):
         @pl.when(place_sub < sub - 1 if step > 0 else place_sub > 0)
         def _(number=number, step=step):
@@ -186,14 +219,20 @@
                     halo_send.at[1 + number], near_recv.at[number], me + step,
                 ).start()
 
-    z_step = block - 2 * block * upper
-    z_target = me + z_step
-    z_send = (z_target >= 0) & (z_target < devices)
-    z_have = (me - z_step >= 0) & (me - z_step < devices)
-    first_turn = ((upper == 0) & (place_sub == 0)) | ((upper == 1) & (place_sub == sub - 1))
-    second_turn = z_have & (
-        ((upper == 0) & (place_sub == sub - 1)) | ((upper == 1) & (place_sub == 0))
-    )
+    near_loads = [
+        pltpu.make_async_copy(blocks.at[leaf], nb.at[leaf], load_sem.at[6])
+        for leaf in range(leaf_dev)
+    ]
+    for copy in near_loads:
+        copy.start()
+
+    two = lift(moment0, leaf_dev // 2)
+    pair2[0, 0] = two[0]
+    pair2[0, 1] = two[1]
+    pair_copy = remote(
+        pair2.at[0], pair2.at[1], p_sem.at[0], p_sem.at[1], me + 1 - 2 * lax.rem(me, 2)
+    )
+    pair_copy.start()
 
     def turn(slot, leaf):
         @pl.when(place_sub == 0)
@@ -210,10 +249,13 @@
                 halo_send.at[4], near_recv.at[0], me - sub + 1,
             ).start()
 
-    def relay_first(leaf):
+    def y_wait(leaf):
         remote(
             buf.at[y_slot, leaf], buf.at[y_slot, leaf], halo_send.at[0], y_recv.at[leaf], across
         ).wait_recv()
+
+    def relay_first(leaf):
+        y_wait(leaf)
 
         @pl.when(z_send)
         def _():
@@ -225,6 +267,21 @@
         @pl.when(first_turn)
         def _():
             turn(y_slot, leaf)
+
+        if leaf >= turned:
+            @pl.when(skip_turn & first_sub)
+            def _():
+                remote(
+                    buf.at[y_slot, leaf], buf.at[3, leaf],
+                    halo_send.at[6], near_recv.at[1], skip_target,
+                ).start()
+
+            @pl.when(skip_turn & last_sub)
+            def _():
+                remote(
+                    buf.at[y_slot, leaf], buf.at[1, leaf],
+                    halo_send.at[6], near_recv.at[0], skip_target,
+                ).start()
 
     def z_wait(leaf):
         remote(
@@ -246,6 +303,8 @@
     def weight(offset, row):
         return jnp.full((rhs, 2 * rank), far_pat[offset, row].astype(F32), F32).astype(BF)
 
+    for copy in small_loads[1:4]:
+        copy.wait()
     c_hi, c_lo = [], []
     for offset in range(3):
         hi, lo = halves(coupling[offset])
@@ -271,6 +330,11 @@
             [jnp.concatenate([hi, hi], axis=1), jnp.concatenate([lo, lo], axis=1)], axis=0
         )
     w_down = jnp.concatenate([wdown[0], wdown[1]], axis=0)
+    if rounds > 0:
+        with mark("06known"):
+            get_known(1)
+        if rounds > 1:
+            make_known(2)
 
     def descend(field, step):
         return fold(nt(split(field), wdown[lax.rem(me >> step, 2)]), rank)
@@ -320,10 +384,11 @@
                 for leaf in late:
                     relay_first(leaf)
 
-    queue = [(relay_first, leaf) for leaf in range(leaf_dev)]
-    queue += [(relay_second, leaf) for leaf in range(leaf_dev)]
-    half = leaf_dev // 2
-    relays(queue[:half], [])
+    ones = [(relay_first, leaf) for leaf in range(leaf_dev)]
+    twos = [(relay_second, leaf) for leaf in range(turned)]
+
+    with mark("07relA"):
+        relays(ones[:head], [])
 
     locals_low = []
     level_vals, level_id = moment0, 0
@@ -342,42 +407,40 @@
         )
         level_id += 1
 
-    for r in range(1, rounds + 1):
-        get_known(r)
-        if r < rounds:
-            make_known(r + 1)
-
-    for k in range(block - 1, 0, -1):
-        source = lax.rem(mine - k + block, block)
-        remote(
-            buf_a.at[source], buf_a.at[source], a_send.at[k], a_recv.at[k], me ^ 1
-        ).wait_recv()
+    with mark("08inner"):
+        pl.when(jnp.logical_not(outer))(send_inner)
+    with mark("09arecv"):
+        pltpu.make_async_copy(
+            buf_a.at[pl.ds(0, block - 1)], buf_a.at[pl.ds(0, block - 1)], a_sem.at[1]
+        ).wait()
     eight = [buf_a[p] for p in range(block)]
     buf6[own_block] = lift(eight, block)[0]
-    b_copies = []
-    for k in range(block_count - 1, 0, -1):
-        b_copies.append(
+    with mark("10known"):
+        for r in range(2, rounds + 1):
+            get_known(r)
+            if r < rounds:
+                make_known(r + 1)
+    with mark("10bsend"):
+        for k in range(block_count - 1, 0, -1):
             remote(
-                buf6.at[own_block], buf6.at[own_block], b_send.at[k], b_recv.at[k],
+                buf6.at[own_block], buf6.at[own_block], b_sem.at[0], b_sem.at[1],
                 lax.rem(own_block + k, block_count) * block + mine,
-            )
-        )
-    for copy in b_copies:
-        copy.start()
+            ).start()
     five = lift(eight, block // 2)
     for p in range(2):
         buf5[p] = five[p]
     q_copy = remote(
-        buf5.at[pl.ds(0, 2)], buf5.at[pl.ds(2, 2)], q_send.at[0], q_recv.at[0],
+        buf5.at[pl.ds(0, 2)], buf5.at[pl.ds(2, 2)], q_sem.at[0], q_sem.at[1],
         (own_block + 1 - 2 * lax.rem(own_block, 2)) * block + mine,
     )
     q_copy.start()
-    pl.when(jnp.logical_not(outer))(send_across)
-    relays(queue[half:leaf_dev], [])
+    with mark("11relC"):
+        relays(ones[head : leaf_dev - 2], [])
     for p, part in enumerate(lift(eight, 2)):
         buf4[p] = part
 
-    pair_copy.wait()
+    with mark("12pair"):
+        pair_copy.wait()
     members2 = two + [pair2[1, 0], pair2[1, 1]]
     groups = [[members2[(c + offset) % 4] for offset in range(1, 4)] for c in range(2)]
     rows = [row_starts[level_id] + me * 2 + c for c in range(2)]
@@ -388,25 +451,26 @@
     rows.append(row_starts[level_id] + me)
     groups.append([buf4[lax.rem(mine // 2 + offset, 4)] for offset in range(1, 4)])
     rows.append(row_starts[level_id + 1] + me // 2)
-    relays(queue[leaf_dev : leaf_dev + 2], range(0, 2))
+    with mark("13relD"):
+        relays(ones[leaf_dev - 2 :] + twos[: turned // 2], [])
     middle = couple(groups, rows)
     locals_low.append(middle[: 2 * rhs])
     field = middle[2 * rhs : 3 * rhs] + descend(middle[3 * rhs :], 0)
     for step in range(len(locals_low) - 1, -1, -1):
         field = locals_low[step] + fan_out(field, rhs)
-    relays(queue[leaf_dev + 2 : leaf_dev + half], range(2, half))
-
-    for copy in near_loads:
-        copy.wait()
-    first = [nt(buf[2, leaf], nb[leaf, 0]) for leaf in range(leaf_dev)]
-    relays(queue[leaf_dev + half :], range(half, leaf_dev))
-
-    for k in range(block_count - 1, 0, -1):
-        source = lax.rem(own_block - k + block_count, block_count)
-        remote(
-            buf6.at[source], buf6.at[source], b_send.at[k], b_recv.at[k], me ^ 1
-        ).wait_recv()
-    q_copy.wait()
+    with mark("14relE"):
+        relays(twos[turned // 2 :], range(relayed))
+
+    with mark("15nearload"):
+        pltpu.make_async_copy(nb, nb, load_sem.at[6]).wait()
+    with mark("16first"):
+        first = [nt(buf[2, leaf], nb[leaf, 0]) for leaf in range(leaf_dev)]
+    with mark("18brecv"):
+        pltpu.make_async_copy(
+            buf6.at[pl.ds(0, block_count - 1)], buf6.at[pl.ds(0, block_count - 1)], b_sem.at[1]
+        ).wait()
+    with mark("19qwait"):
+        q_copy.wait()
     groups = [[buf5[lax.rem(upper + offset, 4)] for offset in range(1, 4)]]
     rows = [row_starts[level_id + 2] + me // sub]
     first_six = level_id + 3
@@ -426,9 +490,10 @@
             buf6[start + span + p] = part
         start, span, level = start + span, span // 2, level + 1
     groups, rows = groups[::-1], rows[::-1]
-    top = split(couple(groups, rows))
-    top = jnp.concatenate([top[p * rhs : (p + 1) * rhs] for p in range(top_count)], axis=1)
-    spread = nn(top, wpath[...])
+    with mark("20top"):
+        top = split(couple(groups, rows))
+        top = jnp.concatenate([top[p * rhs : (p + 1) * rhs] for p in range(top_count)], axis=1)
+        spread = nn(top, wpath[...])
     partial = []
     for leaf in range(leaf_dev):
         whole = split(
@@ -438,35 +503,60 @@
         twice = jnp.concatenate([bas[leaf], bas[leaf]], axis=0)
         partial.append(first[leaf] + nn(whole, twice))
 
-    @pl.when(z_have & jnp.logical_not(second_turn))
-    def _():
+    with mark("21zwait"):
+        @pl.when(jnp.logical_not(outer))
+        def _():
+            for leaf in range(relayed, leaf_dev):
+                y_wait(leaf)
+
+        @pl.when(z_have & jnp.logical_not(second_turn))
+        def _():
+            for leaf in range(turned):
+                z_wait(leaf)
+
+        @pl.when(z_have)
+        def _():
+            for leaf in range(turned, leaf_dev):
+                z_wait(leaf)
+
+    with mark("22near"):
+        for number, step in enumerate((-1, 1)):
+            @pl.when(me > 0 if step < 0 else me < devices - 1)
+            def _(number=number, step=step):
+                pltpu.make_async_copy(
+                    buf.at[2 + step], buf.at[2 + step], near_recv.at[number]
+                ).wait()
+    with mark("23near"):
         for leaf in range(leaf_dev):
-            z_wait(leaf)
-
-    for number, step in enumerate((-1, 1)):
-        @pl.when(me > 0 if step < 0 else me < devices - 1)
-        def _(number=number, step=step):
-            pltpu.make_async_copy(buf.at[2 + step], buf.at[2 + step], near_recv.at[number]).wait()
-    for leaf in range(leaf_dev):
-        acc = partial[leaf]
-        for s in range(1, near):
-            index = near_pat[s, leaf]
-            gap = index // leaf_dev - me
-            place = jnp.where(
-                gap == -sub, 0, jnp.where(gap == -1, 1, jnp.where(gap == 0, 2, jnp.where(gap == 1, 3, 4)))
-            )
-            acc = acc + nt(buf[place, lax.rem(index, leaf_dev)], nb[leaf, s])
-        out[:, points * leaf : points * (leaf + 1)] = acc.astype(out.dtype)
-
+            acc = partial[leaf]
+            for s in range(1, near):
+                index = near_pat[s, leaf]
+                gap = index // leaf_dev - me
+                place = jnp.where(
+                    gap == -sub, 0, jnp.where(gap == -1, 1, jnp.where(gap == 0, 2, jnp.where(gap == 1, 3, 4)))
+                )
+                acc = acc + nt(buf[place, lax.rem(index, leaf_dev)], nb[leaf, s])
+            out[:, points * leaf : points * (leaf + 1)] = acc.astype(out.dtype)
+
+    inner = jnp.logical_not(outer)
     sent = (
-        me >= 0, place_sub < sub - 1, place_sub > 0, z_send, first_turn | second_turn,
-    )
-    for number, condition in enumerate(sent):
+        (0, me >= 0, leaf_dev), (1, place_sub < sub - 1, leaf_dev), (2, place_sub > 0, leaf_dev),
+        (3, z_send & outer, leaf_dev), (3, z_send & inner, relayed),
+        (4, first_turn, leaf_dev), (4, second_turn, turned),
+        (5, z_have & inner, leaf_dev - relayed), (6, skip_turn, leaf_dev - turned),
+    )
+    for number, condition, count in sent:
         @pl.when(condition)
-        def _(number=number):
-            pltpu.make_async_copy(buf.at[2], buf.at[2], halo_send.at[number]).wait()
-    for copy in a_copies + b_copies:
-        copy.wait_send()
+        def _(number=number, count=count):
+            pltpu.make_async_copy(
+                buf.at[2, pl.ds(0, count)], buf.at[2, pl.ds(0, count)], halo_send.at[number]
+            ).wait()
+    pltpu.make_async_copy(
+        buf_a.at[pl.ds(0, block - 1)], buf_a.at[pl.ds(0, block - 1)], a_sem.at[0]
+    ).wait()
+    pltpu.make_async_copy(
+        buf6.at[pl.ds(0, block_count - 1)], buf6.at[pl.ds(0, block_count - 1)], b_sem.at[0]
+    ).wait()
 
 
 def shards(sizes, sources, leaf_basis, transfer, coupling, near_blocks, near_pattern, far_pattern):
@@ -478,13 +568,12 @@
     block_count = devices // block
     top_count = block_count.bit_length() - 1
     vmem = pl.BlockSpec(memory_space=pltpu.VMEM)
-    smem = pl.BlockSpec(memory_space=pltpu.SMEM)
     hbm = pl.BlockSpec(memory_space=pl.ANY)
     dma = pltpu.SemaphoreType.DMA
     result = pl.pallas_call(
         functools.partial(kernel, (sub, devices, leaf_dev, near)),
         out_shape=pltpu.VMEM((rhs, leaf_dev * points), BF),
-        in_specs=[hbm, hbm, vmem, vmem, hbm, smem, smem],
+        in_specs=[hbm] * 7,
         out_specs=vmem,
         scratch_shapes=[
             pltpu.VMEM((5, leaf_dev, rhs, points), BF),
@@ -497,20 +586,19 @@
             pltpu.VMEM((2 * block_count, rhs, 2 * rank), BF),
             pltpu.VMEM((2, 2 * rank, 2 * rank), BF),
             pltpu.VMEM((2 * top_count * rank, 2 * rank * leaf_dev), BF),
-            dma((leaf_dev + 1,)),
-            dma((leaf_dev,)),
-            dma((5,)),
+            pltpu.VMEM(transfer.shape, F32),
+            pltpu.VMEM(coupling.shape, F32),
+            pltpu.SMEM(near_pattern.shape[::-1], jnp.int32),
+            pltpu.SMEM(far_pattern.shape[::-1], jnp.int32),
+            dma((7,)),
+            dma((7,)),
             dma((2,)),
             dma((leaf_dev,)),
             dma((leaf_dev,)),
-            dma((block,)),
-            dma((block,)),
-            dma((1,)),
-            dma((1,)),
-            dma((block_count,)),
-            dma((block_count,)),
-            dma((1,)),
-            dma((1,)),
+            dma((2,)),
+            dma((2,)),
+            dma((2,)),
+            dma((2,)),
             pltpu.SemaphoreType.REGULAR((max(block_count - 2, 1), 2)),
         ],
         compiler_params=pltpu.CompilerParams(collective_id=0, has_side_effects=True),

time: 22.3 us -> 18.9 us (0.85)
  the two profiles are of different devices: /device:TPU:23 before, /device:TPU:15 now
where the time goes in v1:
time: 18.9 us; the launch traced here: 18.5 us
  Pallas kernels  17.8 us (94%)
  local copies, waits for them, and re-layouts  0.71 us (4%)
    pallas_call x1, Pallas kernels, shards(): pl.pallas_call(functools.partial(kernel, (sub, devices, leaf_dev, near)),...  17.8 us
    unnamed x1, local copies, waits for them, and re-layouts  0.71 us

profile of v1, /device:TPU:15, one launch (start us, length us, event | category | flops | bytes accessed | tf_op | source)
XLA Modules:
  0.0 18.5 jit_solution(16441576710234904124)
XLA Ops:
  0.0 17.8 %shard_map.73 = bf16[64,2048]{1,0:T(8,128)(2,1)S(1)} custom-call(bf16[64,2048]{1,0:T(8,128)(2,1)} %bitcast.6, bf16[8,64,256]{2,1,0:T(8,128)(2,1)} %bitcast.7, f32[2,64,64]{2,1,0:T(8,128)} %transfer_hbm.1, f32[3,64,64]{2,1,0:T(8,128)} %coupling_hbm.1, bf16[8,4,256,256]{3,2,1,0:T(8,128)(2,1)} %blocks.1, s32[4,8]{1,0:T(4,128)} %bitcast.9, s32[3,508]{1,0:T(4,128)} %bitcast.8), custom_call_target="tpu_custom_call" | custom-call | tf_op jit(solution)/shard_map/pallas_call | solution.py:573
  17.8 0.7 %copy.9 = bf16[2048,64]{0,1:T(8,128)(2,1)} copy(bf16[2048,64]{0,1:T(8,128)(2,1)S(1)} %bitcast.5) | data formatting | bytes 524288

commit v2 on v1

--- a/solution.py
+++ b/solution.py
@@ -11,6 +11,9 @@
 BF = jnp.bfloat16
 F32 = jnp.float32
 MESH = pl.DeviceIdType.MESH
+PLACE_ONE = (0, 1, 2, 3, 3, 4, 5, 9)
+PLACE_TWO = (6, 6, 7, 8, 9, 9, 10, 10)
+PLACE_INNER = (6, 7, 8, 9, 10, 10, 10, 10)
 
 
 def mark(name):
@@ -38,9 +41,21 @@
     return y[:, :width] + y[:, width:]
 
 
+def relay_plan(leaves, turned, relayed):
+    outer = [[] for _ in range(12)]
+    inner = [[] for _ in range(12)]
+    for leaf in range(leaves):
+        outer[PLACE_ONE[leaf * 8 // leaves]].append((0, leaf))
+    for leaf in range(turned):
+        outer[PLACE_TWO[leaf * 8 // leaves]].append((1, leaf))
+    for leaf in range(relayed):
+        inner[PLACE_INNER[leaf * 8 // leaves]].append(leaf)
+    return outer, inner
+
+
 def kernel(
     cfg, src, basis, transfer_hbm, coupling_hbm, blocks, near_hbm, far_hbm, out,
-    buf, bas, nb, buf_a, pair2, buf4, buf5, buf6, wdown, wpath, transfer, coupling,
+    buf_lo, buf_hi, bas, nb, buf_a, pair2, buf4, buf5, buf6, wdown, wpath, transfer, coupling,
     near_pat, far_pat, load_sem, halo_send, near_recv, y_recv, z_recv, a_sem, p_sem,
     b_sem, q_sem, known,
 ):
@@ -60,7 +75,7 @@
     first_sub, last_sub = place_sub == 0, place_sub == sub - 1
     outer = first_sub | last_sub
     lower = upper == 0
-    relayed = leaf_dev // 2
+    relayed = leaf_dev // 4
     turned = leaf_dev // 2
     head = leaf_dev // 4
 
@@ -119,10 +134,19 @@
     ]
     for copy in small_loads[:1] + small_loads[4:]:
         copy.start()
-    for leaf in range(leaf_dev):
-        pltpu.make_async_copy(
-            src.at[:, pl.ds(points * leaf, points)], buf.at[2, leaf], load_sem.at[5]
-        ).start()
+    bufs = (buf_lo, buf_hi)
+    short = points // 2
+    middle_leaf = leaf_dev // 2
+
+    def piece(slot, number):
+        return bufs[number // middle_leaf].at[slot, pl.ds(2 * (number % middle_leaf), 2)]
+
+    for half in range(2):
+        for leaf in range(leaf_dev):
+            pltpu.make_async_copy(
+                src.at[:, pl.ds(points * leaf + short * half, short)], bufs[half].at[2, leaf],
+                load_sem.at[5 + half],
+            ).start()
     for copy in small_loads[1:4]:
         copy.start()
 
@@ -171,39 +195,41 @@
         lifted = split(fold(nn(rows, w_up[span]), rank))
         return [lifted[p * rhs : (p + 1) * rhs] for p in range(len(parts) // span)]
 
+    def joined(leaf):
+        return jnp.concatenate([buf_lo[2, leaf], buf_hi[2, leaf]], axis=1)
+
     def send_across(leaves):
         for leaf in leaves:
             remote(
-                src.at[:, pl.ds(points * leaf, points)], buf.at[z_slot, leaf],
+                piece(2, leaf), piece(z_slot, leaf),
                 halo_send.at[0], y_recv.at[leaf], across,
             ).start()
 
-    def send_inner():
-        send_across(range(relayed))
-        for leaf in range(relayed, leaf_dev):
-            @pl.when(z_have)
-            def _(leaf=leaf):
-                remote(
-                    src.at[:, pl.ds(points * leaf, points)], buf.at[y_slot, leaf],
-                    halo_send.at[5], z_recv.at[leaf], beyond,
-                ).start()
-
-            send_across([leaf])
-
+    def send_beyond(leaves):
+        for leaf in leaves:
+            remote(
+                piece(2, leaf), piece(y_slot, leaf),
+                halo_send.at[5], z_recv.at[leaf], beyond,
+            ).start()
+
+    with mark("01src"):
+        for half in range(2):
+            pltpu.make_async_copy(
+                bufs[half].at[2], bufs[half].at[2], load_sem.at[5 + half]
+            ).wait()
     with mark("03barrier"):
         pl.semaphore_wait(barrier, expected)
     pl.when(outer)(functools.partial(send_across, range(head)))
     with mark("01load"):
         small_loads[4].wait()
-        pltpu.make_async_copy(buf.at[2], buf.at[2], load_sem.at[5]).wait()
     with mark("02mom"):
-        moment0 = [split(nt(buf[2, leaf], bas[leaf])) for leaf in range(leaf_dev)]
+        moment0 = [split(nt(joined(leaf), bas[leaf])) for leaf in range(leaf_dev)]
         buf_a[mine] = lift(moment0, leaf_dev)[0]
     with mark("04asend"):
-        for k in range(block - 1, 0, -1):
+        for k in [block - 2 * k for k in range(1, block // 2)] + [1]:
             remote(
-                buf_a.at[mine], buf_a.at[mine], a_sem.at[0], a_sem.at[1],
-                own_block * block + lax.rem(mine + k, block),
+                buf_a.at[mine], buf_a.at[mine], a_sem.at[0], a_sem.at[2 if k == 1 else 1],
+                own_block * block + (mine ^ k),
             ).start()
 
     if rounds > 0:
@@ -215,12 +241,12 @@
         def _(number=number, step=step):
             for leaf in range(leaf_dev):
                 remote(
-                    src.at[:, pl.ds(points * leaf, points)], buf.at[2 - step, leaf],
-                    halo_send.at[1 + number], near_recv.at[number], me + step,
+                    piece(2, leaf), piece(2 - step, leaf),
+                    halo_send.at[1 + number], near_recv.at[number, leaf // middle_leaf], me + step,
                 ).start()
 
     near_loads = [
-        pltpu.make_async_copy(blocks.at[leaf], nb.at[leaf], load_sem.at[6])
+        pltpu.make_async_copy(blocks.at[leaf], nb.at[leaf], load_sem.at[7])
         for leaf in range(leaf_dev)
     ]
     for copy in near_loads:
@@ -238,29 +264,30 @@
         @pl.when(place_sub == 0)
         def _():
             remote(
-                buf.at[slot, leaf], buf.at[3, leaf],
-                halo_send.at[4], near_recv.at[1], me + sub - 1,
+                piece(slot, leaf), piece(3, leaf),
+                halo_send.at[4], near_recv.at[1, leaf // middle_leaf], me + sub - 1,
             ).start()
 
         @pl.when(place_sub == sub - 1)
         def _():
             remote(
-                buf.at[slot, leaf], buf.at[1, leaf],
-                halo_send.at[4], near_recv.at[0], me - sub + 1,
+                piece(slot, leaf), piece(1, leaf),
+                halo_send.at[4], near_recv.at[0, leaf // middle_leaf], me - sub + 1,
             ).start()
 
     def y_wait(leaf):
         remote(
-            buf.at[y_slot, leaf], buf.at[y_slot, leaf], halo_send.at[0], y_recv.at[leaf], across
+            piece(y_slot, leaf), piece(y_slot, leaf), halo_send.at[0], y_recv.at[leaf], across
         ).wait_recv()
 
     def relay_first(leaf):
-        y_wait(leaf)
+        with mark(f"y{leaf}"):
+            y_wait(leaf)
 
         @pl.when(z_send)
         def _():
             remote(
-                buf.at[y_slot, leaf], buf.at[z_slot, leaf],
+                piece(y_slot, leaf), piece(z_slot, leaf),
                 halo_send.at[3], z_recv.at[leaf], z_target,
             ).start()
 
@@ -272,26 +299,27 @@
             @pl.when(skip_turn & first_sub)
             def _():
                 remote(
-                    buf.at[y_slot, leaf], buf.at[3, leaf],
-                    halo_send.at[6], near_recv.at[1], skip_target,
+                    piece(y_slot, leaf), piece(3, leaf),
+                    halo_send.at[6], near_recv.at[1, leaf // middle_leaf], skip_target,
                 ).start()
 
             @pl.when(skip_turn & last_sub)
             def _():
                 remote(
-                    buf.at[y_slot, leaf], buf.at[1, leaf],
-                    halo_send.at[6], near_recv.at[0], skip_target,
+                    piece(y_slot, leaf), piece(1, leaf),
+                    halo_send.at[6], near_recv.at[0, leaf // middle_leaf], skip_target,
                 ).start()
 
     def z_wait(leaf):
         remote(
-            buf.at[z_slot, leaf], buf.at[z_slot, leaf], halo_send.at[3], z_recv.at[leaf], across
+            piece(z_slot, leaf), piece(z_slot, leaf), halo_send.at[3], z_recv.at[leaf], across
         ).wait_recv()
 
     def relay_second(leaf):
         @pl.when(second_turn)
         def _():
-            z_wait(leaf)
+            with mark(f"z{leaf}"):
+                z_wait(leaf)
             turn(z_slot, leaf)
 
     row_starts = [0]
@@ -330,12 +358,6 @@
             [jnp.concatenate([hi, hi], axis=1), jnp.concatenate([lo, lo], axis=1)], axis=0
         )
     w_down = jnp.concatenate([wdown[0], wdown[1]], axis=0)
-    if rounds > 0:
-        with mark("06known"):
-            get_known(1)
-        if rounds > 1:
-            make_known(2)
-
     def descend(field, step):
         return fold(nt(split(field), wdown[lax.rem(me >> step, 2)]), rank)
 
@@ -365,30 +387,39 @@
     for leaf in range(leaf_dev):
         for number in range(top_count):
             begin = (leaf * top_count + number) * rank
-            piece = split(chain[begin : begin + rank])
+            both = split(chain[begin : begin + rank])
             for half in range(2):
                 wpath[
                     (2 * number + half) * rank : (2 * number + half + 1) * rank,
                     2 * rank * leaf : 2 * rank * (leaf + 1),
-                ] = piece
-
-    def relays(early, late):
-        @pl.when(outer)
-        def _():
-            for step, leaf in early:
-                step(leaf)
-
+                ] = both
+
+    ones = [(relay_first, leaf) for leaf in range(leaf_dev)]
+    twos = [(relay_second, leaf) for leaf in range(turned)]
+    plan_outer, plan_inner = relay_plan(leaf_dev, turned, relayed)
+
+    def relays(point):
+        early = [ones[leaf] if kind == 0 else twos[leaf] for kind, leaf in plan_outer[point]]
+        if early:
+            @pl.when(outer)
+            def _():
+                for step, leaf in early:
+                    step(leaf)
+
+        late = plan_inner[point]
         if late:
             @pl.when(jnp.logical_not(outer))
             def _():
                 for leaf in late:
                     relay_first(leaf)
 
-    ones = [(relay_first, leaf) for leaf in range(leaf_dev)]
-    twos = [(relay_second, leaf) for leaf in range(turned)]
-
-    with mark("07relA"):
-        relays(ones[:head], [])
+    if rounds > 0:
+        with mark("06known"):
+            get_known(1)
+        if rounds > 1:
+            make_known(2)
+    with mark("07p0"):
+        relays(0)
 
     locals_low = []
     level_vals, level_id = moment0, 0
@@ -406,12 +437,26 @@
             )
         )
         level_id += 1
-
-    with mark("08inner"):
-        pl.when(jnp.logical_not(outer))(send_inner)
-    with mark("09arecv"):
+        if level_id == 1:
+            with mark("08inner"):
+                pl.when(jnp.logical_not(outer))(functools.partial(send_across, range(leaf_dev)))
+            with mark("08p1"):
+                relays(1)
+            with mark("09arecv"):
+                pltpu.make_async_copy(
+                    buf_a.at[pl.ds(0, block // 2 - 1)], buf_a.at[pl.ds(0, block // 2 - 1)],
+                    a_sem.at[1],
+                ).wait()
+            for k in range(2, block, 2):
+                remote(
+                    buf_a.at[mine ^ k], buf_a.at[mine ^ k], a_sem.at[0], a_sem.at[2], me ^ 1
+                ).start()
+
+    with mark("08p2"):
+        relays(2)
+    with mark("09brecv"):
         pltpu.make_async_copy(
-            buf_a.at[pl.ds(0, block - 1)], buf_a.at[pl.ds(0, block - 1)], a_sem.at[1]
+            buf_a.at[pl.ds(0, block // 2)], buf_a.at[pl.ds(0, block // 2)], a_sem.at[2]
         ).wait()
     eight = [buf_a[p] for p in range(block)]
     buf6[own_block] = lift(eight, block)[0]
@@ -421,11 +466,13 @@
             if r < rounds:
                 make_known(r + 1)
     with mark("10bsend"):
-        for k in range(block_count - 1, 0, -1):
+        for k in range(block_count - 1, 1, -1):
             remote(
                 buf6.at[own_block], buf6.at[own_block], b_sem.at[0], b_sem.at[1],
-                lax.rem(own_block + k, block_count) * block + mine,
+                (own_block ^ k) * block + mine,
             ).start()
+    with mark("11p3"):
+        relays(3)
     five = lift(eight, block // 2)
     for p in range(2):
         buf5[p] = five[p]
@@ -434,8 +481,11 @@
         (own_block + 1 - 2 * lax.rem(own_block, 2)) * block + mine,
     )
     q_copy.start()
-    with mark("11relC"):
-        relays(ones[head : leaf_dev - 2], [])
+    pl.when(z_have & jnp.logical_not(outer))(
+        functools.partial(send_beyond, range(relayed, leaf_dev))
+    )
+    with mark("11p4"):
+        relays(4)
     for p, part in enumerate(lift(eight, 2)):
         buf4[p] = part
 
@@ -451,92 +501,131 @@
     rows.append(row_starts[level_id] + me)
     groups.append([buf4[lax.rem(mine // 2 + offset, 4)] for offset in range(1, 4)])
     rows.append(row_starts[level_id + 1] + me // 2)
-    with mark("13relD"):
-        relays(ones[leaf_dev - 2 :] + twos[: turned // 2], [])
+    with mark("13p5"):
+        relays(5)
     middle = couple(groups, rows)
     locals_low.append(middle[: 2 * rhs])
     field = middle[2 * rhs : 3 * rhs] + descend(middle[3 * rhs :], 0)
+    with mark("13p6"):
+        relays(6)
     for step in range(len(locals_low) - 1, -1, -1):
         field = locals_low[step] + fan_out(field, rhs)
-    with mark("14relE"):
-        relays(twos[turned // 2 :], range(relayed))
+        with mark("13p7"):
+            relays(7 + len(locals_low) - 1 - step)
 
     with mark("15nearload"):
-        pltpu.make_async_copy(nb, nb, load_sem.at[6]).wait()
+        pltpu.make_async_copy(nb, nb, load_sem.at[7]).wait()
     with mark("16first"):
-        first = [nt(buf[2, leaf], nb[leaf, 0]) for leaf in range(leaf_dev)]
-    with mark("18brecv"):
-        pltpu.make_async_copy(
-            buf6.at[pl.ds(0, block_count - 1)], buf6.at[pl.ds(0, block_count - 1)], b_sem.at[1]
-        ).wait()
+        first = [nt(joined(leaf), nb[leaf, 0]) for leaf in range(leaf_dev)]
+    with mark("17p10"):
+        relays(10)
     with mark("19qwait"):
         q_copy.wait()
-    groups = [[buf5[lax.rem(upper + offset, 4)] for offset in range(1, 4)]]
-    rows = [row_starts[level_id + 2] + me // sub]
-    first_six = level_id + 3
-    start, span, level = 0, block_count, first_six
-    while True:
-        own = own_block >> (level - first_six)
-        groups.append(
-            [
-                buf6[start + own // 4 * 4 + lax.rem(lax.rem(own, 4) + offset, 4)]
-                for offset in range(1, 4)
-            ]
-        )
-        rows.append(row_starts[level] + own)
-        if span <= 4:
-            break
-        for p, part in enumerate(lift([buf6[start + p] for p in range(span)], 2)):
-            buf6[start + span + p] = part
-        start, span, level = start + span, span // 2, level + 1
-    groups, rows = groups[::-1], rows[::-1]
-    with mark("20top"):
-        top = split(couple(groups, rows))
-        top = jnp.concatenate([top[p * rhs : (p + 1) * rhs] for p in range(top_count)], axis=1)
-        spread = nn(top, wpath[...])
-    partial = []
-    for leaf in range(leaf_dev):
-        whole = split(
-            field[leaf * rhs : (leaf + 1) * rhs]
-            + fold(spread[:, 2 * rank * leaf : 2 * rank * (leaf + 1)], rank)
-        )
-        twice = jnp.concatenate([bas[leaf], bas[leaf]], axis=0)
-        partial.append(first[leaf] + nn(whole, twice))
-
-    with mark("21zwait"):
-        @pl.when(jnp.logical_not(outer))
-        def _():
-            for leaf in range(relayed, leaf_dev):
-                y_wait(leaf)
-
-        @pl.when(z_have & jnp.logical_not(second_turn))
-        def _():
-            for leaf in range(turned):
-                z_wait(leaf)
-
-        @pl.when(z_have)
-        def _():
-            for leaf in range(turned, leaf_dev):
-                z_wait(leaf)
-
-    with mark("22near"):
-        for number, step in enumerate((-1, 1)):
-            @pl.when(me > 0 if step < 0 else me < devices - 1)
-            def _(number=number, step=step):
-                pltpu.make_async_copy(
-                    buf.at[2 + step], buf.at[2 + step], near_recv.at[number]
-                ).wait()
-    with mark("23near"):
+    buf6[own_block ^ 1] = lift([buf5[2], buf5[3]], 2)[0]
+
+    def add_far(base):
+        with mark("18brecv"):
+            pltpu.make_async_copy(
+                buf6.at[pl.ds(0, block_count - 2)], buf6.at[pl.ds(0, block_count - 2)], b_sem.at[1]
+            ).wait()
+        groups = [[buf5[lax.rem(upper + offset, 4)] for offset in range(1, 4)]]
+        rows = [row_starts[level_id + 2] + me // sub]
+        first_six = level_id + 3
+        start, span, level = 0, block_count, first_six
+        while True:
+            own = own_block >> (level - first_six)
+            groups.append(
+                [
+                    buf6[start + own // 4 * 4 + lax.rem(lax.rem(own, 4) + offset, 4)]
+                    for offset in range(1, 4)
+                ]
+            )
+            rows.append(row_starts[level] + own)
+            if span <= 4:
+                break
+            for p, part in enumerate(lift([buf6[start + p] for p in range(span)], 2)):
+                buf6[start + span + p] = part
+            start, span, level = start + span, span // 2, level + 1
+        groups, rows = groups[::-1], rows[::-1]
+        with mark("20top"):
+            top = split(couple(groups, rows))
+            top = jnp.concatenate([top[p * rhs : (p + 1) * rhs] for p in range(top_count)], axis=1)
+            spread = nn(top, wpath[...])
+        partial = []
         for leaf in range(leaf_dev):
-            acc = partial[leaf]
-            for s in range(1, near):
-                index = near_pat[s, leaf]
-                gap = index // leaf_dev - me
-                place = jnp.where(
-                    gap == -sub, 0, jnp.where(gap == -1, 1, jnp.where(gap == 0, 2, jnp.where(gap == 1, 3, 4)))
-                )
-                acc = acc + nt(buf[place, lax.rem(index, leaf_dev)], nb[leaf, s])
-            out[:, points * leaf : points * (leaf + 1)] = acc.astype(out.dtype)
+            whole = split(
+                field[leaf * rhs : (leaf + 1) * rhs]
+                + fold(spread[:, 2 * rank * leaf : 2 * rank * (leaf + 1)], rank)
+            )
+            twice = jnp.concatenate([bas[leaf], bas[leaf]], axis=0)
+            partial.append(base[leaf] + nn(whole, twice))
+        return partial
+
+    def add_near(base):
+        total = base
+        for half in range(2):
+            begin = half * middle_leaf
+            group = range(begin, begin + middle_leaf)
+            with mark(f"21wait{half}"):
+                @pl.when(jnp.logical_not(outer))
+                def _(group=group):
+                    for leaf in group:
+                        if leaf >= relayed:
+                            y_wait(leaf)
+
+                @pl.when(z_have & jnp.logical_not(second_turn))
+                def _(group=group):
+                    for leaf in group:
+                        if leaf < turned:
+                            z_wait(leaf)
+
+                @pl.when(z_have)
+                def _(group=group):
+                    for leaf in group:
+                        if leaf >= turned:
+                            z_wait(leaf)
+
+            with mark(f"22near{half}"):
+                for number, step in enumerate((-1, 1)):
+                    @pl.when(me > 0 if step < 0 else me < devices - 1)
+                    def _(number=number, step=step, half=half):
+                        pltpu.make_async_copy(
+                            bufs[half].at[2 + step], bufs[half].at[2 + step],
+                            near_recv.at[number, half],
+                        ).wait()
+            with mark(f"23sum{half}"):
+                added = []
+                for leaf in range(leaf_dev):
+                    acc = total[leaf]
+                    for s in range(1, near):
+                        index = near_pat[s, leaf]
+                        gap = index // leaf_dev - me
+                        place = jnp.where(
+                            gap == -sub, 0,
+                            jnp.where(
+                                gap == -1, 1,
+                                jnp.where(gap == 0, 2, jnp.where(gap == 1, 3, 4)),
+                            ),
+                        )
+                        acc = acc + nt(
+                            bufs[half][place, lax.rem(index, leaf_dev)],
+                            nb[leaf, s, :, short * half : short * (half + 1)],
+                        )
+                    added.append(acc)
+                total = added
+        return total
+
+    def store(total):
+        for leaf in range(leaf_dev):
+            out[:, points * leaf : points * (leaf + 1)] = total[leaf].astype(out.dtype)
+
+    @pl.when(z_have)
+    def _():
+        store(add_near(add_far(first)))
+
+    @pl.when(jnp.logical_not(z_have))
+    def _():
+        store(add_far(add_near(first)))
 
     inner = jnp.logical_not(outer)
     sent = (
@@ -549,13 +638,14 @@
         @pl.when(condition)
         def _(number=number, count=count):
             pltpu.make_async_copy(
-                buf.at[2, pl.ds(0, count)], buf.at[2, pl.ds(0, count)], halo_send.at[number]
+                src.at[:, pl.ds(0, points * count)], src.at[:, pl.ds(0, points * count)],
+                halo_send.at[number],
             ).wait()
     pltpu.make_async_copy(
         buf_a.at[pl.ds(0, block - 1)], buf_a.at[pl.ds(0, block - 1)], a_sem.at[0]
     ).wait()
     pltpu.make_async_copy(
-        buf6.at[pl.ds(0, block_count - 1)], buf6.at[pl.ds(0, block_count - 1)], b_sem.at[0]
+        buf6.at[pl.ds(0, block_count - 2)], buf6.at[pl.ds(0, block_count - 2)], b_sem.at[0]
     ).wait()
 
 
@@ -576,7 +666,8 @@
         in_specs=[hbm] * 7,
         out_specs=vmem,
         scratch_shapes=[
-            pltpu.VMEM((5, leaf_dev, rhs, points), BF),
+            pltpu.VMEM((5, leaf_dev, rhs, points // 2), BF),
+            pltpu.VMEM((5, leaf_dev, rhs, points // 2), BF),
             pltpu.VMEM((leaf_dev, rank, points), BF),
             pltpu.VMEM((leaf_dev, near, points, points), BF),
             pltpu.VMEM((block, rhs, 2 * rank), BF),
@@ -590,12 +681,12 @@
             pltpu.VMEM(coupling.shape, F32),
             pltpu.SMEM(near_pattern.shape[::-1], jnp.int32),
             pltpu.SMEM(far_pattern.shape[::-1], jnp.int32),
+            dma((8,)),
             dma((7,)),
-            dma((7,)),
-            dma((2,)),
+            dma((2, 2)),
             dma((leaf_dev,)),
             dma((leaf_dev,)),
-            dma((2,)),
+            dma((3,)),
             dma((2,)),
             dma((2,)),
             dma((2,)),

time: 18.9 us -> 17.5 us (0.926); the launches traced: 18.5 us -> 17.3 us
  Pallas kernels: 17.8 us -> 16.6 us
    pallas_call x1, Pallas kernels: 17.8 us -> 16.6 us  [shards(): pl.pallas_call(functools.partial(kernel, (sub, devices, leaf_dev, near)),...]
where the time goes in v2:
time: 17.5 us; the launch traced here: 17.3 us
  Pallas kernels  16.6 us (95%)
  local copies, waits for them, and re-layouts  0.71 us (4%)
    pallas_call x1, Pallas kernels, shards(): pl.pallas_call(functools.partial(kernel, (sub, devices, leaf_dev, near)),...  16.6 us
    unnamed x1, local copies, waits for them, and re-layouts  0.71 us

profile of v2, /device:TPU:15, one launch (start us, length us, event | category | flops | bytes accessed | tf_op | source)
XLA Modules:
  0.0 17.3 jit_solution(2360112433414334682)
XLA Ops:
  0.0 16.6 %shard_map.73 = bf16[64,2048]{1,0:T(8,128)(2,1)S(1)} custom-call(bf16[64,2048]{1,0:T(8,128)(2,1)} %bitcast.6, bf16[8,64,256]{2,1,0:T(8,128)(2,1)} %bitcast.7, f32[2,64,64]{2,1,0:T(8,128)} %transfer_hbm.1, f32[3,64,64]{2,1,0:T(8,128)} %coupling_hbm.1, bf16[8,4,256,256]{3,2,1,0:T(8,128)(2,1)} %blocks.1, s32[4,8]{1,0:T(4,128)} %bitcast.9, s32[3,508]{1,0:T(4,128)} %bitcast.8), custom_call_target="tpu_custom_call" | custom-call | tf_op jit(solution)/shard_map/pallas_call | solution.py:663
  16.6 0.7 %copy.9 = bf16[2048,64]{0,1:T(8,128)(2,1)} copy(bf16[2048,64]{0,1:T(8,128)(2,1)S(1)} %bitcast.5) | data formatting | bytes 524288

commit v3 on v2

--- a/solution.py
+++ b/solution.py
@@ -11,8 +11,8 @@
 BF = jnp.bfloat16
 F32 = jnp.float32
 MESH = pl.DeviceIdType.MESH
-PLACE_ONE = (0, 1, 2, 3, 3, 4, 5, 9)
-PLACE_TWO = (6, 6, 7, 8, 9, 9, 10, 10)
+PLACE_ONE = (0, 1, 2, 3, 3, 4, 5, 6)
+PLACE_TWO = (6, 7, 8, 9, 10, 10, 10, 10)
 PLACE_INNER = (6, 7, 8, 9, 10, 10, 10, 10)
 
 
@@ -55,9 +55,8 @@
 
 def kernel(
     cfg, src, basis, transfer_hbm, coupling_hbm, blocks, near_hbm, far_hbm, out,
-    buf_lo, buf_hi, bas, nb, buf_a, pair2, buf4, buf5, buf6, wdown, wpath, transfer, coupling,
-    near_pat, far_pat, load_sem, halo_send, near_recv, y_recv, z_recv, a_sem, p_sem,
-    b_sem, q_sem, known,
+    buf_lo, buf_hi, bas, nb, moment, buf_a, pair2, buf4, buf5, buf6, wdown, wpath, transfer, coupling,
+    near_pat, far_pat, load_sem, sent_sem, near_recv, y_recv, z_recv, a_recv, far_recv, known,
 ):
     sub, devices, leaf_dev, near = cfg
     rank = basis.shape[1]
@@ -75,7 +74,9 @@
     first_sub, last_sub = place_sub == 0, place_sub == sub - 1
     outer = first_sub | last_sub
     lower = upper == 0
-    relayed = leaf_dev // 4
+    early = lower & (place_sub < sub // 2)
+    relayed = leaf_dev // 8
+    kept = leaf_dev
     turned = leaf_dev // 2
     head = leaf_dev // 4
 
@@ -123,17 +124,15 @@
     greet(barrier, z_have, beyond)
     greet(barrier, z_have & first_turn, skip_source)
 
+    first_load = pltpu.make_async_copy(transfer_hbm, transfer, load_sem.at[0])
+    base_load = pltpu.make_async_copy(basis, bas, load_sem.at[1])
+    first_load.start()
+    base_load.start()
     small_loads = [
-        pltpu.make_async_copy(source, dest, load_sem.at[number])
-        for number, (source, dest) in enumerate(
-            (
-                (transfer_hbm, transfer), (coupling_hbm, coupling),
-                (near_hbm, near_pat), (far_hbm, far_pat), (basis, bas),
-            )
-        )
+        pltpu.make_async_copy(coupling_hbm, coupling, load_sem.at[1]),
+        pltpu.make_async_copy(near_hbm, near_pat, load_sem.at[2]),
+        pltpu.make_async_copy(far_hbm, far_pat, load_sem.at[3]),
     ]
-    for copy in small_loads[:1] + small_loads[4:]:
-        copy.start()
     bufs = (buf_lo, buf_hi)
     short = points // 2
     middle_leaf = leaf_dev // 2
@@ -145,10 +144,8 @@
         for leaf in range(leaf_dev):
             pltpu.make_async_copy(
                 src.at[:, pl.ds(points * leaf + short * half, short)], bufs[half].at[2, leaf],
-                load_sem.at[5 + half],
+                load_sem.at[2 + half],
             ).start()
-    for copy in small_loads[1:4]:
-        copy.start()
 
     rounds = block_count - 2
 
@@ -173,7 +170,7 @@
         return jnp.concatenate(rows, axis=0)
 
     with mark("00tc"):
-        small_loads[0].wait()
+        first_load.wait()
     sides = [transfer[side] for side in range(2)]
     step_weight = jnp.concatenate([doubled([side]) for side in sides], axis=1)
     w_up = {2: doubled(sides)}
@@ -202,33 +199,42 @@
         for leaf in leaves:
             remote(
                 piece(2, leaf), piece(z_slot, leaf),
-                halo_send.at[0], y_recv.at[leaf], across,
+                sent_sem.at[0], y_recv.at[leaf], across,
             ).start()
 
     def send_beyond(leaves):
         for leaf in leaves:
             remote(
                 piece(2, leaf), piece(y_slot, leaf),
-                halo_send.at[5], z_recv.at[leaf], beyond,
+                sent_sem.at[0], z_recv.at[min(leaf, turned)], beyond,
             ).start()
 
     with mark("01src"):
         for half in range(2):
             pltpu.make_async_copy(
-                bufs[half].at[2], bufs[half].at[2], load_sem.at[5 + half]
+                bufs[half].at[2], bufs[half].at[2], load_sem.at[2 + half]
             ).wait()
+        base_load.wait()
+    for copy in small_loads:
+        copy.start()
+
+    def find_moments():
+        parts = [split(nt(joined(leaf), bas[leaf])) for leaf in range(leaf_dev)]
+        for leaf in range(leaf_dev):
+            moment[leaf] = parts[leaf]
+        buf_a[mine] = lift(parts, leaf_dev)[0]
+
+    with mark("02early"):
+        pl.when(early)(find_moments)
     with mark("03barrier"):
         pl.semaphore_wait(barrier, expected)
     pl.when(outer)(functools.partial(send_across, range(head)))
-    with mark("01load"):
-        small_loads[4].wait()
     with mark("02mom"):
-        moment0 = [split(nt(joined(leaf), bas[leaf])) for leaf in range(leaf_dev)]
-        buf_a[mine] = lift(moment0, leaf_dev)[0]
+        pl.when(jnp.logical_not(early))(find_moments)
     with mark("04asend"):
         for k in [block - 2 * k for k in range(1, block // 2)] + [1]:
             remote(
-                buf_a.at[mine], buf_a.at[mine], a_sem.at[0], a_sem.at[2 if k == 1 else 1],
+                buf_a.at[mine], buf_a.at[mine], sent_sem.at[0], a_recv.at[1 if k == 1 else 0],
                 own_block * block + (mine ^ k),
             ).start()
 
@@ -242,21 +248,22 @@
             for leaf in range(leaf_dev):
                 remote(
                     piece(2, leaf), piece(2 - step, leaf),
-                    halo_send.at[1 + number], near_recv.at[number, leaf // middle_leaf], me + step,
+                    sent_sem.at[0], near_recv.at[number, leaf // middle_leaf], me + step,
                 ).start()
 
     near_loads = [
-        pltpu.make_async_copy(blocks.at[leaf], nb.at[leaf], load_sem.at[7])
+        pltpu.make_async_copy(blocks.at[leaf], nb.at[leaf], load_sem.at[0])
         for leaf in range(leaf_dev)
     ]
     for copy in near_loads:
         copy.start()
 
+    moment0 = [moment[leaf] for leaf in range(leaf_dev)]
     two = lift(moment0, leaf_dev // 2)
     pair2[0, 0] = two[0]
     pair2[0, 1] = two[1]
     pair_copy = remote(
-        pair2.at[0], pair2.at[1], p_sem.at[0], p_sem.at[1], me + 1 - 2 * lax.rem(me, 2)
+        pair2.at[0], pair2.at[1], sent_sem.at[0], far_recv.at[0], me + 1 - 2 * lax.rem(me, 2)
     )
     pair_copy.start()
 
@@ -265,31 +272,32 @@
         def _():
             remote(
                 piece(slot, leaf), piece(3, leaf),
-                halo_send.at[4], near_recv.at[1, leaf // middle_leaf], me + sub - 1,
+                sent_sem.at[0], near_recv.at[1, leaf // middle_leaf], me + sub - 1,
             ).start()
 
         @pl.when(place_sub == sub - 1)
         def _():
             remote(
                 piece(slot, leaf), piece(1, leaf),
-                halo_send.at[4], near_recv.at[0, leaf // middle_leaf], me - sub + 1,
+                sent_sem.at[0], near_recv.at[0, leaf // middle_leaf], me - sub + 1,
             ).start()
 
     def y_wait(leaf):
         remote(
-            piece(y_slot, leaf), piece(y_slot, leaf), halo_send.at[0], y_recv.at[leaf], across
+            piece(y_slot, leaf), piece(y_slot, leaf), sent_sem.at[0], y_recv.at[leaf], across
         ).wait_recv()
 
     def relay_first(leaf):
         with mark(f"y{leaf}"):
             y_wait(leaf)
 
-        @pl.when(z_send)
-        def _():
-            remote(
-                piece(y_slot, leaf), piece(z_slot, leaf),
-                halo_send.at[3], z_recv.at[leaf], z_target,
-            ).start()
+        if leaf < kept:
+            @pl.when(z_send)
+            def _():
+                remote(
+                    piece(y_slot, leaf), piece(z_slot, leaf),
+                    sent_sem.at[0], z_recv.at[min(leaf, turned)], z_target,
+                ).start()
 
         @pl.when(first_turn)
         def _():
@@ -300,19 +308,19 @@
             def _():
                 remote(
                     piece(y_slot, leaf), piece(3, leaf),
-                    halo_send.at[6], near_recv.at[1, leaf // middle_leaf], skip_target,
+                    sent_sem.at[0], near_recv.at[1, leaf // middle_leaf], skip_target,
                 ).start()
 
             @pl.when(skip_turn & last_sub)
             def _():
                 remote(
                     piece(y_slot, leaf), piece(1, leaf),
-                    halo_send.at[6], near_recv.at[0, leaf // middle_leaf], skip_target,
+                    sent_sem.at[0], near_recv.at[0, leaf // middle_leaf], skip_target,
                 ).start()
 
     def z_wait(leaf):
         remote(
-            piece(z_slot, leaf), piece(z_slot, leaf), halo_send.at[3], z_recv.at[leaf], across
+            piece(z_slot, leaf), piece(z_slot, leaf), sent_sem.at[0], z_recv.at[leaf], across
         ).wait_recv()
 
     def relay_second(leaf):
@@ -331,7 +339,7 @@
     def weight(offset, row):
         return jnp.full((rhs, 2 * rank), far_pat[offset, row].astype(F32), F32).astype(BF)
 
-    for copy in small_loads[1:4]:
+    for copy in small_loads:
         copy.wait()
     c_hi, c_lo = [], []
     for offset in range(3):
@@ -445,18 +453,18 @@
             with mark("09arecv"):
                 pltpu.make_async_copy(
                     buf_a.at[pl.ds(0, block // 2 - 1)], buf_a.at[pl.ds(0, block // 2 - 1)],
-                    a_sem.at[1],
+                    a_recv.at[0],
                 ).wait()
             for k in range(2, block, 2):
                 remote(
-                    buf_a.at[mine ^ k], buf_a.at[mine ^ k], a_sem.at[0], a_sem.at[2], me ^ 1
+                    buf_a.at[mine ^ k], buf_a.at[mine ^ k], sent_sem.at[0], a_recv.at[1], me ^ 1
                 ).start()
 
     with mark("08p2"):
         relays(2)
     with mark("09brecv"):
         pltpu.make_async_copy(
-            buf_a.at[pl.ds(0, block // 2)], buf_a.at[pl.ds(0, block // 2)], a_sem.at[2]
+            buf_a.at[pl.ds(0, block // 2)], buf_a.at[pl.ds(0, block // 2)], a_recv.at[1]
         ).wait()
     eight = [buf_a[p] for p in range(block)]
     buf6[own_block] = lift(eight, block)[0]
@@ -468,7 +476,7 @@
     with mark("10bsend"):
         for k in range(block_count - 1, 1, -1):
             remote(
-                buf6.at[own_block], buf6.at[own_block], b_sem.at[0], b_sem.at[1],
+                buf6.at[own_block], buf6.at[own_block], sent_sem.at[0], far_recv.at[1],
                 (own_block ^ k) * block + mine,
             ).start()
     with mark("11p3"):
@@ -477,20 +485,22 @@
     for p in range(2):
         buf5[p] = five[p]
     q_copy = remote(
-        buf5.at[pl.ds(0, 2)], buf5.at[pl.ds(2, 2)], q_sem.at[0], q_sem.at[1],
+        buf5.at[pl.ds(0, 2)], buf5.at[pl.ds(2, 2)], sent_sem.at[0], far_recv.at[2],
         (own_block + 1 - 2 * lax.rem(own_block, 2)) * block + mine,
     )
     q_copy.start()
     pl.when(z_have & jnp.logical_not(outer))(
         functools.partial(send_beyond, range(relayed, leaf_dev))
     )
+    if kept < leaf_dev:
+        pl.when(z_have & outer)(functools.partial(send_beyond, range(kept, leaf_dev)))
     with mark("11p4"):
         relays(4)
     for p, part in enumerate(lift(eight, 2)):
         buf4[p] = part
 
     with mark("12pair"):
-        pair_copy.wait()
+        pair_copy.wait_recv()
     members2 = two + [pair2[1, 0], pair2[1, 1]]
     groups = [[members2[(c + offset) % 4] for offset in range(1, 4)] for c in range(2)]
     rows = [row_starts[level_id] + me * 2 + c for c in range(2)]
@@ -514,19 +524,19 @@
             relays(7 + len(locals_low) - 1 - step)
 
     with mark("15nearload"):
-        pltpu.make_async_copy(nb, nb, load_sem.at[7]).wait()
+        pltpu.make_async_copy(nb, nb, load_sem.at[0]).wait()
     with mark("16first"):
         first = [nt(joined(leaf), nb[leaf, 0]) for leaf in range(leaf_dev)]
     with mark("17p10"):
         relays(10)
     with mark("19qwait"):
-        q_copy.wait()
+        q_copy.wait_recv()
     buf6[own_block ^ 1] = lift([buf5[2], buf5[3]], 2)[0]
 
     def add_far(base):
         with mark("18brecv"):
             pltpu.make_async_copy(
-                buf6.at[pl.ds(0, block_count - 2)], buf6.at[pl.ds(0, block_count - 2)], b_sem.at[1]
+                buf6.at[pl.ds(0, block_count - 2)], buf6.at[pl.ds(0, block_count - 2)], far_recv.at[1]
             ).wait()
         groups = [[buf5[lax.rem(upper + offset, 4)] for offset in range(1, 4)]]
         rows = [row_starts[level_id + 2] + me // sub]
@@ -579,11 +589,14 @@
                         if leaf < turned:
                             z_wait(leaf)
 
-                @pl.when(z_have)
-                def _(group=group):
-                    for leaf in group:
-                        if leaf >= turned:
-                            z_wait(leaf)
+                if half:
+                    @pl.when(z_have)
+                    def _():
+                        count = leaf_dev - turned
+                        pltpu.make_async_copy(
+                            src.at[:, pl.ds(0, points * count)], src.at[:, pl.ds(0, points * count)],
+                            z_recv.at[turned],
+                        ).wait()
 
             with mark(f"22near{half}"):
                 for number, step in enumerate((-1, 1)):
@@ -630,23 +643,28 @@
     inner = jnp.logical_not(outer)
     sent = (
         (0, me >= 0, leaf_dev), (1, place_sub < sub - 1, leaf_dev), (2, place_sub > 0, leaf_dev),
-        (3, z_send & outer, leaf_dev), (3, z_send & inner, relayed),
+        (3, z_send & outer, kept), (3, z_send & inner, relayed),
         (4, first_turn, leaf_dev), (4, second_turn, turned),
-        (5, z_have & inner, leaf_dev - relayed), (6, skip_turn, leaf_dev - turned),
+        (5, z_have & inner, leaf_dev - relayed), (5, z_have & outer, leaf_dev - kept), (6, skip_turn, leaf_dev - turned),
     )
     for number, condition, count in sent:
+        if count == 0:
+            continue
+
         @pl.when(condition)
         def _(number=number, count=count):
             pltpu.make_async_copy(
                 src.at[:, pl.ds(0, points * count)], src.at[:, pl.ds(0, points * count)],
-                halo_send.at[number],
+                sent_sem.at[0],
             ).wait()
     pltpu.make_async_copy(
-        buf_a.at[pl.ds(0, block - 1)], buf_a.at[pl.ds(0, block - 1)], a_sem.at[0]
+        buf_a.at[pl.ds(0, block - 1)], buf_a.at[pl.ds(0, block - 1)], sent_sem.at[0]
     ).wait()
     pltpu.make_async_copy(
-        buf6.at[pl.ds(0, block_count - 2)], buf6.at[pl.ds(0, block_count - 2)], b_sem.at[0]
+        buf6.at[pl.ds(0, block_count - 2)], buf6.at[pl.ds(0, block_count - 2)], sent_sem.at[0]
     ).wait()
+    pair_copy.wait_send()
+    q_copy.wait_send()
 
 
 def shards(sizes, sources, leaf_basis, transfer, coupling, near_blocks, near_pattern, far_pattern):
@@ -670,6 +688,7 @@
             pltpu.VMEM((5, leaf_dev, rhs, points // 2), BF),
             pltpu.VMEM((leaf_dev, rank, points), BF),
             pltpu.VMEM((leaf_dev, near, points, points), BF),
+            pltpu.VMEM((leaf_dev, rhs, 2 * rank), BF),
             pltpu.VMEM((block, rhs, 2 * rank), BF),
             pltpu.VMEM((2, 2, rhs, 2 * rank), BF),
             pltpu.VMEM((4, rhs, 2 * rank), BF),
@@ -681,15 +700,13 @@
             pltpu.VMEM(coupling.shape, F32),
             pltpu.SMEM(near_pattern.shape[::-1], jnp.int32),
             pltpu.SMEM(far_pattern.shape[::-1], jnp.int32),
-            dma((8,)),
-            dma((7,)),
+            dma((4,)),
+            dma((1,)),
             dma((2, 2)),
             dma((leaf_dev,)),
-            dma((leaf_dev,)),
+            dma((leaf_dev // 2 + 1,)),
+            dma((2,)),
             dma((3,)),
-            dma((2,)),
-            dma((2,)),
-            dma((2,)),
             pltpu.SemaphoreType.REGULAR((max(block_count - 2, 1), 2)),
         ],
         compiler_params=pltpu.CompilerParams(collective_id=0, has_side_effects=True),

time: 17.5 us -> 16.5 us (0.943)
  Pallas kernels: 16.6 us -> 15.6 us
    pallas_call x1, Pallas kernels: 16.6 us -> 15.6 us  [shards(): pl.pallas_call(functools.partial(kernel, (sub, devices, leaf_dev, near)),...]
where the time goes in v3:
time: 16.5 us; the launch traced here: 16.3 us
  Pallas kernels  15.6 us (95%)
  local copies, waits for them, and re-layouts  0.71 us (4%)
    pallas_call x1, Pallas kernels, shards(): pl.pallas_call(functools.partial(kernel, (sub, devices, leaf_dev, near)),...  15.6 us
    unnamed x1, local copies, waits for them, and re-layouts  0.71 us

profile of v3, /device:TPU:15, one launch (start us, length us, event | category | flops | bytes accessed | tf_op | source)
XLA Modules:
  0.0 16.3 jit_solution(18307408364112624701)
XLA Ops:
  0.0 15.6 %shard_map.73 = bf16[64,2048]{1,0:T(8,128)(2,1)S(1)} custom-call(bf16[64,2048]{1,0:T(8,128)(2,1)} %bitcast.6, bf16[8,64,256]{2,1,0:T(8,128)(2,1)} %bitcast.7, f32[2,64,64]{2,1,0:T(8,128)} %transfer_hbm.1, f32[3,64,64]{2,1,0:T(8,128)} %coupling_hbm.1, bf16[8,4,256,256]{3,2,1,0:T(8,128)(2,1)} %blocks.1, s32[4,8]{1,0:T(4,128)} %bitcast.9, s32[3,508]{1,0:T(4,128)} %bitcast.8), custom_call_target="tpu_custom_call" | custom-call | tf_op jit(solution)/shard_map/pallas_call | solution.py:681
  15.6 0.7 %copy.9 = bf16[2048,64]{0,1:T(8,128)(2,1)} copy(bf16[2048,64]{0,1:T(8,128)(2,1)S(1)} %bitcast.5) | data formatting | bytes 524288

commit v4 on v3

--- a/solution.py
+++ b/solution.py
@@ -56,7 +56,7 @@
 def kernel(
     cfg, src, basis, transfer_hbm, coupling_hbm, blocks, near_hbm, far_hbm, out,
     buf_lo, buf_hi, bas, nb, moment, buf_a, pair2, buf4, buf5, buf6, wdown, wpath, transfer, coupling,
-    near_pat, far_pat, load_sem, sent_sem, near_recv, y_recv, z_recv, a_recv, far_recv, known,
+    near_pat, far_pat, load_sem, sent_sem, near_recv, y_recv, z_recv, a_recv, far_recv, known, told,
 ):
     sub, devices, leaf_dev, near = cfg
     rank = basis.shape[1]
@@ -74,7 +74,10 @@
     first_sub, last_sub = place_sub == 0, place_sub == sub - 1
     outer = first_sub | last_sub
     lower = upper == 0
-    early = lower & (place_sub < sub // 2)
+    reach = sub // 2
+    early = lower & (place_sub < reach)
+    corner = jnp.logical_not(lower) & (place_sub >= reach)
+    guide = lower & (place_sub >= reach)
     relayed = leaf_dev // 8
     kept = leaf_dev
     turned = leaf_dev // 2
@@ -114,11 +117,12 @@
         def _():
             pl.semaphore_signal(semaphore, inc=1, device_id=target(peer), device_id_type=MESH)
 
-    expected = len(peers) + sum(
+    expected = len(peers) - jnp.where(early, reach, 0) + sum(
         jnp.where(condition, 1, 0) for condition in (has_prev, has_next, z_have, skip_turn)
     )
     for peer in peers:
-        pl.semaphore_signal(barrier, inc=1, device_id=target(peer), device_id_type=MESH)
+        place = lax.rem(peer, block)
+        greet(barrier, jnp.logical_not(corner & (place < reach)), peer)
     greet(barrier, has_prev, me - block)
     greet(barrier, has_next, me + block)
     greet(barrier, z_have, beyond)
@@ -225,14 +229,20 @@
         buf_a[mine] = lift(parts, leaf_dev)[0]
 
     with mark("02early"):
-        pl.when(early)(find_moments)
+        pl.when(early & jnp.logical_not(has_prev))(find_moments)
     with mark("03barrier"):
         pl.semaphore_wait(barrier, expected)
+    greet(told.at[0], guide, me - reach)
     pl.when(outer)(functools.partial(send_across, range(head)))
     with mark("02mom"):
-        pl.when(jnp.logical_not(early))(find_moments)
+        pl.when(jnp.logical_not(early & jnp.logical_not(has_prev)))(find_moments)
     with mark("04asend"):
-        for k in [block - 2 * k for k in range(1, block // 2)] + [1]:
+        for k in [*range(2, block - 2, 2), 1, block - 2]:
+            if k == block - 2:
+                @pl.when(early)
+                def _():
+                    pl.semaphore_wait(told.at[0], 1)
+
             remote(
                 buf_a.at[mine], buf_a.at[mine], sent_sem.at[0], a_recv.at[1 if k == 1 else 0],
                 own_block * block + (mine ^ k),
@@ -446,20 +456,18 @@
         )
         level_id += 1
         if level_id == 1:
-            with mark("08inner"):
-                pl.when(jnp.logical_not(outer))(functools.partial(send_across, range(leaf_dev)))
+            pl.when(jnp.logical_not(outer))(functools.partial(send_across, range(leaf_dev)))
             with mark("08p1"):
                 relays(1)
-            with mark("09arecv"):
-                pltpu.make_async_copy(
-                    buf_a.at[pl.ds(0, block // 2 - 1)], buf_a.at[pl.ds(0, block // 2 - 1)],
-                    a_recv.at[0],
-                ).wait()
-            for k in range(2, block, 2):
-                remote(
-                    buf_a.at[mine ^ k], buf_a.at[mine ^ k], sent_sem.at[0], a_recv.at[1], me ^ 1
-                ).start()
-
+    with mark("09arecv"):
+        pltpu.make_async_copy(
+            buf_a.at[pl.ds(0, block // 2 - 1)], buf_a.at[pl.ds(0, block // 2 - 1)],
+            a_recv.at[0],
+        ).wait()
+    for k in range(2, block, 2):
+        remote(
+            buf_a.at[mine ^ k], buf_a.at[mine ^ k], sent_sem.at[0], a_recv.at[1], me ^ 1
+        ).start()
     with mark("08p2"):
         relays(2)
     with mark("09brecv"):
@@ -708,6 +716,7 @@
             dma((2,)),
             dma((3,)),
             pltpu.SemaphoreType.REGULAR((max(block_count - 2, 1), 2)),
+            pltpu.SemaphoreType.REGULAR((1,)),
         ],
         compiler_params=pltpu.CompilerParams(collective_id=0, has_side_effects=True),
     )(

time: 16.5 us -> 16.4 us (level)
  Pallas kernels: 15.6 us -> 15.4 us
    pallas_call x1, Pallas kernels: 15.6 us -> 15.4 us  [shards(): pl.pallas_call(functools.partial(kernel, (sub, devices, leaf_dev, near)),...]
where the time goes in v4:
time: 16.4 us; the launch traced here: 16.2 us
  Pallas kernels  15.4 us (94%)
  local copies, waits for them, and re-layouts  0.71 us (4%)
    pallas_call x1, Pallas kernels, shards(): pl.pallas_call(functools.partial(kernel, (sub, devices, leaf_dev, near)),...  15.4 us
    unnamed x1, local copies, waits for them, and re-layouts  0.71 us

profile of v4, /device:TPU:15, one launch (start us, length us, event | category | flops | bytes accessed | tf_op | source)
XLA Modules:
  0.0 16.2 jit_solution(6303847408460846780)
XLA Ops:
  0.0 15.4 %shard_map.73 = bf16[64,2048]{1,0:T(8,128)(2,1)S(1)} custom-call(bf16[64,2048]{1,0:T(8,128)(2,1)} %bitcast.6, bf16[8,64,256]{2,1,0:T(8,128)(2,1)} %bitcast.7, f32[2,64,64]{2,1,0:T(8,128)} %transfer_hbm.1, f32[3,64,64]{2,1,0:T(8,128)} %coupling_hbm.1, bf16[8,4,256,256]{3,2,1,0:T(8,128)(2,1)} %blocks.1, s32[4,8]{1,0:T(4,128)} %bitcast.9, s32[3,508]{1,0:T(4,128)} %bitcast.8), custom_call_target="tpu_custom_call" | custom-call | tf_op jit(solution)/shard_map/pallas_call | solution.py:689
  15.5 0.7 %copy.9 = bf16[2048,64]{0,1:T(8,128)(2,1)} copy(bf16[2048,64]{0,1:T(8,128)(2,1)S(1)} %bitcast.5) | data formatting | bytes 524288

commit v5 on v4

--- a/solution.py
+++ b/solution.py
@@ -80,7 +80,7 @@
     guide = lower & (place_sub >= reach)
     relayed = leaf_dev // 8
     kept = leaf_dev
-    turned = leaf_dev // 2
+    turned = leaf_dev // 2 + 1
     head = leaf_dev // 4
 
     y_slot = 4 - 4 * upper
@@ -470,6 +470,9 @@
         ).start()
     with mark("08p2"):
         relays(2)
+    pl.when(z_have & jnp.logical_not(outer))(
+        functools.partial(send_beyond, range(relayed, 3))
+    )
     with mark("09brecv"):
         pltpu.make_async_copy(
             buf_a.at[pl.ds(0, block // 2)], buf_a.at[pl.ds(0, block // 2)], a_recv.at[1]
@@ -498,7 +501,7 @@
     )
     q_copy.start()
     pl.when(z_have & jnp.logical_not(outer))(
-        functools.partial(send_beyond, range(relayed, leaf_dev))
+        functools.partial(send_beyond, range(3, leaf_dev))
     )
     if kept < leaf_dev:
         pl.when(z_have & outer)(functools.partial(send_beyond, range(kept, leaf_dev)))
@@ -712,7 +715,7 @@
             dma((1,)),
             dma((2, 2)),
             dma((leaf_dev,)),
-            dma((leaf_dev // 2 + 1,)),
+            dma((leaf_dev // 2 + 2,)),
             dma((2,)),
             dma((3,)),
             pltpu.SemaphoreType.REGULAR((max(block_count - 2, 1), 2)),

time: 16.4 us -> 16.3 us (level)
  no operation moved by 1% of the time
where the time goes in v5:
time: 16.3 us; the launch traced here: 16.2 us
  Pallas kernels  15.5 us (95%)
  local copies, waits for them, and re-layouts  0.71 us (4%)
    pallas_call x1, Pallas kernels, shards(): pl.pallas_call(functools.partial(kernel, (sub, devices, leaf_dev, near)),...  15.5 us
    unnamed x1, local copies, waits for them, and re-layouts  0.71 us

profile of v5, /device:TPU:15, one launch (start us, length us, event | category | flops | bytes accessed | tf_op | source)
XLA Modules:
  0.0 16.2 jit_solution(8341297890713477044)
XLA Ops:
  0.0 15.5 %shard_map.73 = bf16[64,2048]{1,0:T(8,128)(2,1)S(1)} custom-call(bf16[64,2048]{1,0:T(8,128)(2,1)} %bitcast.6, bf16[8,64,256]{2,1,0:T(8,128)(2,1)} %bitcast.7, f32[2,64,64]{2,1,0:T(8,128)} %transfer_hbm.1, f32[3,64,64]{2,1,0:T(8,128)} %coupling_hbm.1, bf16[8,4,256,256]{3,2,1,0:T(8,128)(2,1)} %blocks.1, s32[4,8]{1,0:T(4,128)} %bitcast.9, s32[3,508]{1,0:T(4,128)} %bitcast.8), custom_call_target="tpu_custom_call" | custom-call | tf_op jit(solution)/shard_map/pallas_call | solution.py:692
  15.5 0.7 %copy.9 = bf16[2048,64]{0,1:T(8,128)(2,1)} copy(bf16[2048,64]{0,1:T(8,128)(2,1)S(1)} %bitcast.5) | data formatting | bytes 524288

commit v6 on v5

--- a/solution.py
+++ b/solution.py
@@ -11,6 +11,7 @@
 BF = jnp.bfloat16
 F32 = jnp.float32
 MESH = pl.DeviceIdType.MESH
+PLACE_EARLY = (1, 1, 2, 3, 4, 4, 5, 6)
 PLACE_ONE = (0, 1, 2, 3, 3, 4, 5, 6)
 PLACE_TWO = (6, 7, 8, 9, 10, 10, 10, 10)
 PLACE_INNER = (6, 7, 8, 9, 10, 10, 10, 10)
@@ -42,15 +43,15 @@
 
 
 def relay_plan(leaves, turned, relayed):
-    outer = [[] for _ in range(12)]
-    inner = [[] for _ in range(12)]
+    outer, soon, inner = ([[] for _ in range(12)] for _ in range(3))
     for leaf in range(leaves):
         outer[PLACE_ONE[leaf * 8 // leaves]].append((0, leaf))
+        soon[PLACE_EARLY[leaf * 8 // leaves]].append((0, leaf))
     for leaf in range(turned):
         outer[PLACE_TWO[leaf * 8 // leaves]].append((1, leaf))
     for leaf in range(relayed):
         inner[PLACE_INNER[leaf * 8 // leaves]].append(leaf)
-    return outer, inner
+    return outer, soon, inner
 
 
 def kernel(
@@ -414,15 +415,22 @@
 
     ones = [(relay_first, leaf) for leaf in range(leaf_dev)]
     twos = [(relay_second, leaf) for leaf in range(turned)]
-    plan_outer, plan_inner = relay_plan(leaf_dev, turned, relayed)
+    plan_outer, plan_soon, plan_inner = relay_plan(leaf_dev, turned, relayed)
 
     def relays(point):
-        early = [ones[leaf] if kind == 0 else twos[leaf] for kind, leaf in plan_outer[point]]
-        if early:
-            @pl.when(outer)
+        steps = [ones[leaf] if kind == 0 else twos[leaf] for kind, leaf in plan_outer[point]]
+        soon = [leaf for _, leaf in plan_soon[point]]
+        if steps:
+            @pl.when(outer & jnp.logical_not(early))
             def _():
-                for step, leaf in early:
+                for step, leaf in steps:
                     step(leaf)
+
+        if soon:
+            @pl.when(outer & early)
+            def _():
+                for leaf in soon:
+                    relay_first(leaf)
 
         late = plan_inner[point]
         if late:

time: 16.3 us -> 16.3 us (level)
  no operation moved by 1% of the time
where the time goes in v6:
time: 16.3 us; the launch traced here: 16.2 us
  Pallas kernels  15.5 us (95%)
  local copies, waits for them, and re-layouts  0.71 us (4%)
    pallas_call x1, Pallas kernels, shards(): pl.pallas_call(functools.partial(kernel, (sub, devices, leaf_dev, near)),...  15.5 us
    unnamed x1, local copies, waits for them, and re-layouts  0.71 us

profile of v6, /device:TPU:15, one launch (start us, length us, event | category | flops | bytes accessed | tf_op | source)
XLA Modules:
  0.0 16.2 jit_solution(3723455743265724025)
XLA Ops:
  0.0 15.5 %shard_map.73 = bf16[64,2048]{1,0:T(8,128)(2,1)S(1)} custom-call(bf16[64,2048]{1,0:T(8,128)(2,1)} %bitcast.6, bf16[8,64,256]{2,1,0:T(8,128)(2,1)} %bitcast.7, f32[2,64,64]{2,1,0:T(8,128)} %transfer_hbm.1, f32[3,64,64]{2,1,0:T(8,128)} %coupling_hbm.1, bf16[8,4,256,256]{3,2,1,0:T(8,128)(2,1)} %blocks.1, s32[4,8]{1,0:T(4,128)} %bitcast.9, s32[3,508]{1,0:T(4,128)} %bitcast.8), custom_call_target="tpu_custom_call" | custom-call | tf_op jit(solution)/shard_map/pallas_call | solution.py:700
  15.5 0.7 %copy.9 = bf16[2048,64]{0,1:T(8,128)(2,1)} copy(bf16[2048,64]{0,1:T(8,128)(2,1)S(1)} %bitcast.5) | data formatting | bytes 524288
